TPU v7x, 128 devices: a whole 4x4x4 slice. The times are simulated.
128 devices in a mesh: blk: 16 (over z, y), slab: 2 (over x_hi), micro: 4 (over x_lo, core).
Axes of the slice: x: 4 (x_hi: 2, x_lo: 2; x = x_hi * 2 + x_lo), y: 4, z: 4, core: 2. Of those that a mesh axis runs over, the one named last changes fastest.
Arguments:
- displacement: float32 [128, 128, 256], P('blk', 'micro', 'slab'), may hold values from -6 to 6
- load_field: float32 [128, 128, 256], P('blk', 'micro', 'slab'), may hold values from -6 to 6
- foundation: float32 [128, 128, 256], P('blk', 'micro', 'slab'), may hold values from 0.2 to 2
- plastic_flags: int32 [128, 128, 256], P('blk', 'micro', 'slab'), may hold values 0 or 1
- point_slot: int32 [128, 128, 256], P('blk', 'micro', 'slab'), may hold values from 0 to 65535, as said below
- family_in: float32 [4, 3, 256], replicated, may hold values from -5 to 5
- family_mid: bfloat16 [4, 256, 256], replicated, may hold values from -0.375 to 0.375
- family_out: bfloat16 [4, 3, 256], replicated, may hold values from -0.375 to 0.375
- family_tan: float32 [4, 256], replicated, may hold values from 0.002 to 0.02
Outputs:
- updated_field: float32 [128, 128, 256], P('blk', 'micro', 'slab')
- solver_residual: float32 [128, 128, 256], P('blk', 'micro', 'slab')
Inputs may be any that keep to these rules, and one draw needn't show every extreme that they name: `point_slot`: within each device's block of 8 x 32 x 128 nodes the values are distinct; value // 16384 is the point's fibre family and value % 16384 its position among that family's points of the block in node order (last dimension fastest); in every block one family holds exactly 16384 points.
All inputs are finite; a program needn't handle non-finite values. No bound on the sum of `plastic_flags` on one device may be relied on, other than what follows from the above.
Results may differ from a plain program's by a relative error of at most 0.0024.
Values sent between devices are 32-bit elements; how exact they have to be, the bound alone decides.
A program may use at most 128 MiB of HBM per device.

v0:
```python
import jax
import jax.numpy as jnp
from jax import lax
from jax.sharding import PartitionSpec as P

ITERS = 8


def padded_2(cells, sides, width, closed):
    for axis, dim in sides:
        count = lax.axis_size(axis)
        ends = count if closed else count - 1
        head = lax.slice_in_dim(cells, 0, width, axis=dim)
        tail = lax.slice_in_dim(cells, cells.shape[dim] - width, cells.shape[dim], axis=dim)
        cells = jnp.concatenate(
            [
                lax.ppermute(tail, axis, [(i, (i + 1) % count) for i in range(ends)]),
                cells,
                lax.ppermute(head, axis, [((i + 1) % count, i) for i in range(ends)]),
            ],
            axis=dim,
        )
    return cells


def shifted_diff(extended, dim_index, halo_width, margin, length):
    upper_side = lax.slice_in_dim(
        extended, halo_width - margin + 1, halo_width + length + margin + 1, axis=dim_index
    )
    lower_side = lax.slice_in_dim(
        extended, halo_width - margin - 1, halo_width + length + margin - 1, axis=dim_index
    )
    return (upper_side - lower_side) * 0.5


def extend(stacked, halo_width):
    cycle_ext = padded_2(stacked, (("blk", 1),), halo_width, True)
    slab_ext = padded_2(stacked, (("slab", 3), ("micro", 2)), halo_width, False)
    return (cycle_ext, slab_ext)


def gradients(stacked, halo_width, margin):
    size_x, size_y, size_z = stacked.shape[1:]
    cycle_ext, slab_ext = extend(stacked, halo_width)
    along_x = shifted_diff(cycle_ext, 1, halo_width, margin, size_x)
    along_y = shifted_diff(
        lax.slice_in_dim(slab_ext, halo_width, halo_width + size_z, axis=3),
        2,
        halo_width,
        margin,
        size_y,
    )
    along_z = shifted_diff(
        lax.slice_in_dim(slab_ext, halo_width, halo_width + size_y, axis=2),
        3,
        halo_width,
        margin,
        size_z,
    )
    return (along_x, along_y, along_z)


def fibre_model(block_rows, weight_in, weight_mid, weight_out, weight_tan):
    modal = (
        weight_in[0][:, None] * block_rows[0][None, :]
        + weight_in[1][:, None] * block_rows[1][None, :]
        + weight_in[2][:, None] * block_rows[2][None, :]
    )
    active = jnp.where(block_rows[3][None, :] > 0.5, jnp.tanh(modal), modal).astype(jnp.bfloat16)
    hidden = jnp.dot(weight_mid, active, preferred_element_type=jnp.float32)
    bounded = jnp.tanh(hidden).astype(jnp.bfloat16)
    stress = jnp.dot(weight_out, bounded, preferred_element_type=jnp.float32)
    widened = bounded.astype(jnp.float32)
    tangent = 0.5 + jnp.dot(weight_tan, widened * widened, precision=lax.Precision.HIGHEST)
    return jnp.concatenate([stress, tangent[None, :]], axis=0)


def global_sum(value):
    return lax.psum(value, ("blk", "slab", "micro"))


def body(
    displacement,
    load_field,
    foundation,
    plastic_flags,
    point_slot,
    family_in,
    family_mid,
    family_out,
    family_tan,
):
    size_x, size_y, size_z = displacement.shape
    points_dev = size_x * size_y * size_z
    capacity = points_dev // 2
    family_count = family_in.shape[0]
    strain_x, strain_y, strain_z = gradients(displacement[None], 1, 0)
    payload = jnp.concatenate(
        [strain_x, strain_y, strain_z, plastic_flags[None].astype(jnp.float32)], axis=0
    ).reshape(4, points_dev)
    slots = point_slot.reshape(points_dev)
    padded = (
        jnp.zeros((4, family_count * capacity), jnp.float32)
        .at[:, slots]
        .set(payload)
        .reshape(4, family_count, capacity)
    )
    per_family = lax.map(
        lambda inputs: fibre_model(inputs[0], inputs[1], inputs[2], inputs[3], inputs[4]),
        (jnp.moveaxis(padded, 1, 0), family_in, family_mid, family_out, family_tan),
    )
    returned = jnp.moveaxis(per_family, 0, 1)
    answers = returned.reshape(4, family_count * capacity)[:, slots].reshape(
        4, size_x, size_y, size_z
    )
    cycle_ext, slab_ext = extend(answers, 1)
    stress_x = shifted_diff(cycle_ext[0], 0, 1, 0, size_x)
    stress_y = shifted_diff(slab_ext[1][:, :, 1 : 1 + size_z], 1, 1, 0, size_y)
    stress_z = shifted_diff(slab_ext[2][:, 1 : 1 + size_y, :], 2, 1, 0, size_z)
    tangent_x = cycle_ext[3]
    tangent_y = slab_ext[3][:, :, 1 : 1 + size_z]
    tangent_z = slab_ext[3][:, 1 : 1 + size_y, :]
    rhs = load_field - foundation * displacement + (stress_x + stress_y + stress_z)
    solution = jnp.zeros_like(rhs)
    residual = rhs
    direction = rhs
    current = global_sum(jnp.sum(residual * residual))
    for iteration in range(ITERS):
        grad_x, grad_y, grad_z = gradients(direction[None], 2, 1)
        flux_x = tangent_x * grad_x[0]
        flux_y = tangent_y * grad_y[0]
        flux_z = tangent_z * grad_z[0]
        total = (
            shifted_diff(flux_x, 0, 1, 0, size_x)
            + shifted_diff(flux_y, 1, 1, 0, size_y)
            + shifted_diff(flux_z, 2, 1, 0, size_z)
        )
        image = foundation * direction - total
        alpha = current / global_sum(jnp.sum(direction * image))
        solution = solution + alpha * direction
        residual = residual - alpha * image
        following = global_sum(jnp.sum(residual * residual))
        direction = residual + following / current * direction
        current = following
    return (displacement + solution, residual)


def solution(mesh):
    placed = (
        P("blk", "micro", "slab"),
        P("blk", "micro", "slab"),
        P("blk", "micro", "slab"),
        P("blk", "micro", "slab"),
        P("blk", "micro", "slab"),
        P(),
        P(),
        P(),
        P(),
    )
    return jax.shard_map(
        body,
        mesh=mesh,
        in_specs=placed,
        out_specs=(P("blk", "micro", "slab"), P("blk", "micro", "slab")),
        check_vma=False,
    )
```

profile of v0, /device:TPU:0, one launch (start us, length us, event | category | flops | bytes accessed | tf_op | source)
XLA Modules:
  0.0 1534.9 jit_solution(5746683782115413864)
XLA Ops:
  8.8 6.5 collective-permute-start
  25.6 8.4 copy.40
  34.0 93.5 %scatter_custom_fusion = f32[4,65536]{0,1:T(8,128)} fusion(s32[32768]{0:T(1024)S(1)} %bitcast.213, f32[32768,4]{1,0:T(8,128)} %copy.40, f32[]{:T(128)} %constant.13.clone.1), kind=kCustom, calls=%fused_computation.34 | custom fusion | bytes 1049088 | tf_op jit(solution)/shard_map/scatter | solution.py:105
  127.5 18.1 %copy.41 = f32[4,4,16384]{2,0,1:T(4,128)S(1)} copy(f32[4,4,16384]{0,2,1:T(8,128)} %bitcast.150) | data formatting | bytes 2097152 | tf_op jit(solution)/shard_map/reshape | solution.py:106
  145.5 78.6 %while.10 = (s32[]{:T(128)}, f32[4,4,16384]{2,1,0:T(4,128)S(1)}, bf16[4,3,256]{2,1,0:T(4,128)(2,1)S(1)}, bf16[4,256,256]{2,1,0:T(8,128)(2,1)}, f32[4,4,16384]{2,...) while((s32[]{:T(128)}, f32[4,4,16384]{2,1,0:T(4,128)S(1)}, ...), condition=%wide.region_2.3_spmd, body=%wide.region_1.2_spmd.sunk | while | flops 2265022464 | bytes 26981568 | solution.py:108
  146.9 7.5 fusion.180
  155.5 9.5 fusion.181
  166.4 7.5 fusion.180
  175.0 9.5 fusion.181
  185.9 7.5 fusion.180
  194.5 9.5 fusion.181
  205.4 7.5 fusion.180
  214.0 9.5 fusion.181
  224.1 16.1 %copy.43 = f32[4,4,16384]{0,2,1:T(8,128)} copy(f32[4,4,16384]{2,0,1:T(4,128)S(1)} %bitcast.211) | data formatting | bytes 2097152 | tf_op jit(solution)/shard_map/transpose | solution.py:112
  240.2 119.1 %gather_fusion = f32[32768,4]{1,0:T(8,128)} fusion(f32[4,65536]{0,1:T(8,128)} %bitcast.151, s32[32768]{0:T(1024)S(1)} %broadcast_clamp_fusion), kind=kCustom, calls=%fused_computation | custom fusion | bytes 1179648 | tf_op jit(solution)/shard_map/gather | solution.py:113
  359.2 10.0 copy.45
  376.8 10.8 collective-permute-done.8
  426.7 62.8 %all-reduce = (f32[]{:T(128)}, f32[]{:T(128)}) all-reduce(f32[]{:T(128)} %get-tuple-element.55, f32[]{:T(128)} %get-tuple-element.54), channel_id=1, replica_groups=mesh['blk'=16,'slab'=2,'micro'=4] {'blk','slab','micro'}, use_global_device_ids=true, to_apply=%region_4.5 | all-reduce | flops 2 | bytes 16 | tf_op jit(solution)/shard_map/psum | solution.py:79
  491.5 64.6 %psum.114 = f32[]{:T(128)} all-reduce(f32[]{:T(128)} %multiply_reduce_fusion.13), channel_id=1, replica_groups=mesh['blk'=16,'slab'=2,'micro'=4] {'blk','slab','micro'}, use_global_device_ids=true, to_apply=%region_8.9 | all-reduce | flops 1 | bytes 8 | tf_op jit(solution)/shard_map/psum | solution.py:79
  576.0 63.5 %psum.115 = f32[]{:T(128)} all-reduce(f32[]{:T(128)} %get-tuple-element.96), channel_id=1, replica_groups=mesh['blk'=16,'slab'=2,'micro'=4] {'blk','slab','micro'}, use_global_device_ids=true, to_apply=%region_10.11 | all-reduce | flops 1 | bytes 8 | tf_op jit(solution)/shard_map/psum | solution.py:79
  641.5 62.4 %psum.116 = f32[]{:T(128)} all-reduce(f32[]{:T(128)} %get-tuple-element.94), channel_id=1, replica_groups=mesh['blk'=16,'slab'=2,'micro'=4] {'blk','slab','micro'}, use_global_device_ids=true, to_apply=%region_12.13 | all-reduce | flops 1 | bytes 8 | tf_op jit(solution)/shard_map/psum | solution.py:79
  723.9 63.6 %psum.117 = f32[]{:T(128)} all-reduce(f32[]{:T(128)} %get-tuple-element.92), channel_id=1, replica_groups=mesh['blk'=16,'slab'=2,'micro'=4] {'blk','slab','micro'}, use_global_device_ids=true, to_apply=%region_14.15 | all-reduce | flops 1 | bytes 8 | tf_op jit(solution)/shard_map/psum | solution.py:79
  789.5 64.1 %psum.118 = f32[]{:T(128)} all-reduce(f32[]{:T(128)} %get-tuple-element.90), channel_id=1, replica_groups=mesh['blk'=16,'slab'=2,'micro'=4] {'blk','slab','micro'}, use_global_device_ids=true, to_apply=%region_16.17 | all-reduce | flops 1 | bytes 8 | tf_op jit(solution)/shard_map/psum | solution.py:79
  873.4 63.9 %psum.119 = f32[]{:T(128)} all-reduce(f32[]{:T(128)} %get-tuple-element.88), channel_id=1, replica_groups=mesh['blk'=16,'slab'=2,'micro'=4] {'blk','slab','micro'}, use_global_device_ids=true, to_apply=%region_18.19 | all-reduce | flops 1 | bytes 8 | tf_op jit(solution)/shard_map/psum | solution.py:79
  939.2 62.3 %psum.120 = f32[]{:T(128)} all-reduce(f32[]{:T(128)} %get-tuple-element.86), channel_id=1, replica_groups=mesh['blk'=16,'slab'=2,'micro'=4] {'blk','slab','micro'}, use_global_device_ids=true, to_apply=%region_20.21 | all-reduce | flops 1 | bytes 8 | tf_op jit(solution)/shard_map/psum | solution.py:79
  1021.4 64.1 %psum.121 = f32[]{:T(128)} all-reduce(f32[]{:T(128)} %get-tuple-element.84), channel_id=1, replica_groups=mesh['blk'=16,'slab'=2,'micro'=4] {'blk','slab','micro'}, use_global_device_ids=true, to_apply=%region_22.23 | all-reduce | flops 1 | bytes 8 | tf_op jit(solution)/shard_map/psum | solution.py:79
  1087.4 63.8 %psum.122 = f32[]{:T(128)} all-reduce(f32[]{:T(128)} %get-tuple-element.82), channel_id=1, replica_groups=mesh['blk'=16,'slab'=2,'micro'=4] {'blk','slab','micro'}, use_global_device_ids=true, to_apply=%region_24.25 | all-reduce | flops 1 | bytes 8 | tf_op jit(solution)/shard_map/psum | solution.py:79
  1170.9 64.0 %psum.123 = f32[]{:T(128)} all-reduce(f32[]{:T(128)} %get-tuple-element.80), channel_id=1, replica_groups=mesh['blk'=16,'slab'=2,'micro'=4] {'blk','slab','micro'}, use_global_device_ids=true, to_apply=%region_26.27 | all-reduce | flops 1 | bytes 8 | tf_op jit(solution)/shard_map/psum | solution.py:79
  1236.9 62.2 %psum.124 = f32[]{:T(128)} all-reduce(f32[]{:T(128)} %get-tuple-element.78), channel_id=1, replica_groups=mesh['blk'=16,'slab'=2,'micro'=4] {'blk','slab','micro'}, use_global_device_ids=true, to_apply=%region_28.29 | all-reduce | flops 1 | bytes 8 | tf_op jit(solution)/shard_map/psum | solution.py:79
  1318.9 64.2 %psum.125 = f32[]{:T(128)} all-reduce(f32[]{:T(128)} %get-tuple-element.76), channel_id=1, replica_groups=mesh['blk'=16,'slab'=2,'micro'=4] {'blk','slab','micro'}, use_global_device_ids=true, to_apply=%region_30.31 | all-reduce | flops 1 | bytes 8 | tf_op jit(solution)/shard_map/psum | solution.py:79
  1385.1 63.8 %psum.126 = f32[]{:T(128)} all-reduce(f32[]{:T(128)} %get-tuple-element.74), channel_id=1, replica_groups=mesh['blk'=16,'slab'=2,'micro'=4] {'blk','slab','micro'}, use_global_device_ids=true, to_apply=%region_32.33 | all-reduce | flops 1 | bytes 8 | tf_op jit(solution)/shard_map/psum | solution.py:79
  1468.6 63.9 %psum.127 = f32[]{:T(128)} all-reduce(f32[]{:T(128)} %get-tuple-element.72), channel_id=1, replica_groups=mesh['blk'=16,'slab'=2,'micro'=4] {'blk','slab','micro'}, use_global_device_ids=true, to_apply=%region_34.35 | all-reduce | flops 1 | bytes 8 | tf_op jit(solution)/shard_map/psum | solution.py:79
  (234 shorter events, 208.8 us)
Async XLA Ops:
  1.7 14.6 collective-permute-start.2
  6.8 9.6 collective-permute-start.3
  8.8 14.5 collective-permute-start
  15.3 8.0 collective-permute-start.1
  369.4 18.2 %collective-permute-start.8 = (f32[4,8,32,1]{3,2,1,0:T(8,128)S(1)}, f32[4,8,32,1]{3,2,1,0:T(8,128)S(1)}, u32[]{:S(2)}, u32[]{:S(2)}) collective-permute-start(f32[4,8,32,1]{3,2,1,0:T(8,128)S(1)} %get-tuple-element.114), channel_id=1, source_target_pairs={{0,4},{1,5},{2,6},{3,7},{8,12},{9,13},{10,14},{11,15},{16,20},{17,... | collective-permute-start | bytes 12296 | tf_op jit(solution)/shard_map/ppermute | solution.py:17
  375.5 17.8 %collective-permute-start.9 = (f32[4,8,32,1]{3,2,1,0:T(8,128)S(1)}, f32[4,8,32,1]{3,2,1,0:T(8,128)S(1)}, u32[]{:S(2)}, u32[]{:S(2)}) collective-permute-start(f32[4,8,32,1]{3,2,1,0:T(8,128)S(1)} %get-tuple-element.115), channel_id=1, source_target_pairs={{4,0},{5,1},{6,2},{7,3},{12,8},{13,9},{14,10},{15,11},{20,16},{21,... | collective-permute-start | bytes 12296 | tf_op jit(solution)/shard_map/ppermute | solution.py:19
  393.6 8.3 collective-permute-start.10
  401.9 8.2 collective-permute-start.7
  411.8 8.6 collective-permute-start.15
  413.1 12.8 collective-permute-start.12
  413.2 12.7 collective-permute-start.13
  561.3 8.4 collective-permute-start.21
  562.6 12.5 collective-permute-start.18
  564.1 11.1 collective-permute-start.19
  709.3 8.4 collective-permute-start.27
  710.6 12.6 collective-permute-start.24
  712.2 11.0 collective-permute-start.25
  858.7 8.4 collective-permute-start.33
  860.1 12.5 collective-permute-start.30
  861.7 10.9 collective-permute-start.31
  1006.7 8.4 collective-permute-start.39
  1008.0 12.6 collective-permute-start.36
  1009.7 10.9 collective-permute-start.37
  1156.3 8.4 collective-permute-start.45
  1157.6 12.5 collective-permute-start.42
  1159.3 10.9 collective-permute-start.43
  1304.3 8.4 collective-permute-start.51
  1305.6 12.6 collective-permute-start.48
  1307.5 10.7 collective-permute-start.49
  1454.0 8.4 collective-permute-start.57
  1455.3 12.5 collective-permute-start.54
  1457.0 10.9 collective-permute-start.55
  (31 other events, 656.9 us)
where the time goes:
time: 1550 us; the launch traced here: 1530 us
  blocking collectives  953 us (61%)
  local copies, waits for them, and re-layouts  272 us (18%)
  starting transfers between devices  122 us (8%)
  matrix products  72.6 us (5%)
  waiting for transfers between devices  69.2 us (4%)
  other arithmetic  22.7 us (1%)
  between operations  22 us (1%)
    psum x15, blocking collectives, global_sum(): return lax.psum(value, ('blk', 'slab', 'micro'))  953 us
    gather x1, local copies, waits for them, and re-layouts, body(): returned.reshape(4, family_count * capacity)[:, slots]  119 us
    scatter x1, local copies, waits for them, and re-layouts, body(): padded = jnp.zeros((4, family_count * capacity), jnp.float32).at[:, slots...  93.5 us
    ppermute x30, starting transfers between devices, padded_2(): lax.ppermute(tail, axis, [(i, (i + 1) % count) for i in range(ends)])  73 us
    ppermute x30, starting transfers between devices, padded_2(): lax.ppermute(head, axis, [((i + 1) % count, i) for i in range(ends)])  49.3 us
    ppermute x30, waiting for transfers between devices, padded_2(): lax.ppermute(head, axis, [((i + 1) % count, i) for i in range(ends)])  47.2 us
    dot_general x4, matrix products, fibre_model(): jnp.dot(weight_tan, widened * widened, precision=lax.Precision.HIGHEST)  37.9 us
  transfers between devices with their start and end apart: 60, of which 20 were waited for; matrix products, arithmetic and copies ran while one was open for 1% of the time, Pallas kernels for 0%

commit v1 on v0

v1 whole, which is shorter than its diff:
```python
import jax
import jax.numpy as jnp
from jax import lax
from jax.experimental import pallas as pl
from jax.experimental.pallas import tpu as pltpu
from jax.sharding import PartitionSpec as P

F32 = jnp.float32
BF16 = jnp.bfloat16
MESH = pl.DeviceIdType.MESH
FAMILIES = 4
MODES = 256
CAP_SHIFT = 14
ROWS = 16
SIGMA = 3.0
NX, NY, NZ = 8, 32, 128
TILES = NY // 8
E_DISP, E_TAN, E_SX, E_SY, E_R, E_W, E_T = 0, 1, 2, 3, 4, 5, 6
N_EX = 12
N_RED = 4
N_DOT = 13


def prepare_weights(family_in, family_mid, family_out, family_tan, w_in, w_mid, w_out):
    zero = jnp.zeros((1, MODES), F32)
    high, low, stress, tangent = [], [], [], []
    for f in range(FAMILIES):
        weight = family_in[f]
        rounded = weight.astype(BF16).astype(F32)
        high += [rounded, rounded, zero, zero]
        low += [weight - rounded, zero, zero, zero, zero, zero]
        w_mid[:, f * MODES : (f + 1) * MODES] = family_mid[f]
        tan = family_tan[f : f + 1, :]
        tan_high = tan.astype(BF16).astype(F32)
        stress += [family_out[f].astype(F32)] + [zero] * 5
        tangent += [zero] * 3 + [tan_high, tan - tan_high] + [zero] * 3
    w_in[...] = jnp.concatenate(high + low, axis=0).T.astype(BF16)
    w_out[:, :MODES] = jnp.concatenate(stress, axis=0).astype(BF16)
    w_out[:, MODES:] = jnp.concatenate(tangent, axis=0).astype(BF16)


def fibre_chunk(points, w_in, w_mid, w_out, base):
    width = ROWS * NZ
    rows = jnp.concatenate([points[pl.ds(base + 8 * i, 8), :] for i in range(ROWS)], axis=1)
    family, flag = rows[6:7, :], rows[7:8, :]
    family_8 = jnp.broadcast_to(family, (8, width))
    chosen = [family_8 == float(f) for f in range(FAMILIES)]
    strain = jnp.concatenate([jnp.where(m, rows, 0.0) for m in chosen], axis=0).astype(BF16)
    modal = jnp.dot(w_in[...], jnp.concatenate([strain, strain], axis=0), preferred_element_type=F32)
    modal = modal.reshape(MODES // 8, 8, width)
    plastic = jnp.broadcast_to(flag, (8, width)) > 0.5
    active = jnp.where(plastic[None], jnp.tanh(modal), modal).reshape(MODES, width).astype(BF16)
    active = active.reshape(MODES // 16, 16, width)
    family_16 = jnp.broadcast_to(family, (16, width))
    parts = []
    for f in range(FAMILIES):
        mask = jnp.where(family_16 == float(f), 1.0, 0.0).astype(BF16)
        parts.append((active * mask[None]).reshape(MODES, width))
    hidden = jnp.dot(w_mid[...], jnp.concatenate(parts, axis=0), preferred_element_type=F32)
    bounded = jnp.tanh(hidden).astype(BF16)
    out = jnp.dot(
        w_out[...], jnp.concatenate([bounded, bounded * bounded], axis=0), preferred_element_type=F32
    )
    picked = jnp.where(
        chosen[0], out[0:8], jnp.where(chosen[1], out[8:16], jnp.where(chosen[2], out[16:24], out[24:32]))
    )
    for i in range(ROWS):
        points[pl.ds(base + 8 * i, 8), :] = picked[:, i * NZ : (i + 1) * NZ]


def newton_kernel(
    disp_ref, load_ref, found_ref, flags_ref, slot_ref, fin_ref, fmid_ref, fout_ref, ftan_ref,
    field_out, residual_out,
    ex, zsend, zrecv, red, points, w_in, w_mid, w_out, coef, s_z,
    x_, r_, w_, z_, z2_, p_, s_, t_, u_, v_,
    send_sem, recv_sem, red_send, red_recv,
):
    blk, slab, micro = lax.axis_index("blk"), lax.axis_index("slab"), lax.axis_index("micro")
    n_blk = lax.axis_size("blk")
    up_blk, down_blk = lax.rem(blk + 1, n_blk), lax.rem(blk + n_blk - 1, n_blk)
    part_x = slab * 4 + micro
    part_y, part_z = lax.rem(blk, 4), lax.div(blk, 4)

    def peer_x(step):
        other = lax.rem(part_x + step, 8)
        return (blk, lax.div(other, 4), lax.rem(other, 4))

    def peer_y(step):
        return (part_z * 4 + lax.rem(part_y + step, 4), slab, micro)

    def peer_z(step):
        return (lax.rem(part_z + step, 4) * 4 + part_y, slab, micro)

    barrier = pltpu.get_barrier_semaphore()
    friends = [peer_x(j) for j in range(1, 8)] + [peer_y(j) for j in range(1, 4)]
    friends += [peer_z(j) for j in range(1, 4)] + [(up_blk, slab, micro), (down_blk, slab, micro)]
    for friend in friends:
        pl.semaphore_signal(barrier, inc=1, device_id=friend, device_id_type=MESH)

    lane = lax.broadcasted_iota(jnp.int32, (8, NZ), 1)
    first_slab, last_slab = slab == 0, slab == 1
    pack_id = lax.shift_right_logical(lax.rem(lane + 2 * (1 - slab), NZ), 1)
    edge_up = {n: jnp.logical_and(lane < n, first_slab) for n in (1, 2)}
    edge_down = {n: jnp.logical_and(lane >= NZ - n, last_slab) for n in (1, 2)}

    def keep(condition):
        return jnp.where(condition, 0.0, 1.0).astype(F32)

    keep_up_1 = keep(jnp.logical_and(lane == NZ - 1, last_slab))[None]
    keep_down_1 = keep(jnp.logical_and(lane == 0, first_slab))[None]
    keep_up_2 = keep(jnp.logical_and(lane >= NZ - 2, last_slab))[None]
    keep_down_2 = keep(jnp.logical_and(lane < 2, first_slab))[None]

    @pl.when(micro == 0)
    def _():
        for e in range(N_EX):
            ex[e, :, 0:8, :] = jnp.zeros((NX + 4, 8, NZ), F32)

    @pl.when(micro == 3)
    def _():
        for e in range(N_EX):
            ex[e, :, NY + 8 : NY + 16, :] = jnp.zeros((NX + 4, 8, NZ), F32)

    def copy(source, target, e, k, device):
        return pltpu.make_async_remote_copy(
            src_ref=source, dst_ref=target, send_sem=send_sem.at[e, k], recv_sem=recv_sem.at[e, k],
            device_id=device, device_id_type=MESH,
        )

    def copies_x(e, depth):
        up = copy(
            ex.at[e, pl.ds(NX + 2 - depth, depth), pl.ds(8, NY), :],
            ex.at[e, pl.ds(2 - depth, depth), pl.ds(8, NY), :], e, 0, (up_blk, slab, micro),
        )
        down = copy(
            ex.at[e, pl.ds(2, depth), pl.ds(8, NY), :],
            ex.at[e, pl.ds(NX + 2, depth), pl.ds(8, NY), :], e, 1, (down_blk, slab, micro),
        )
        return up, down

    def copies_y(e):
        up = copy(
            ex.at[e, pl.ds(2, NX), pl.ds(NY, 8), :], ex.at[e, pl.ds(2, NX), pl.ds(0, 8), :],
            e, 2, (blk, slab, lax.rem(micro + 1, 4)),
        )
        down = copy(
            ex.at[e, pl.ds(2, NX), pl.ds(8, 8), :], ex.at[e, pl.ds(2, NX), pl.ds(NY + 8, 8), :],
            e, 3, (blk, slab, lax.rem(micro + 3, 4)),
        )
        return up, down

    def copy_z(e):
        return copy(zsend.at[e], zrecv.at[e], e, 4, (blk, 1 - slab, micro))

    def start(e, depth, x=True, y=True, z=True):
        if x:
            for c in copies_x(e, depth):
                c.start()
        if z:
            copy_z(e).start()
        if y:
            up, down = copies_y(e)

            @pl.when(micro < 3)
            def _():
                up.start()

            @pl.when(micro > 0)
            def _():
                down.start()

    def finish(e, depth, x=True, y=True, z=True):
        if x:
            for c in copies_x(e, depth):
                c.wait_recv()
        if z:
            copy_z(e).wait_recv()
        if y:
            up, down = copies_y(e)

            @pl.when(micro > 0)
            def _():
                up.wait_recv()

            @pl.when(micro < 3)
            def _():
                down.wait_recv()

    def drain(e, depth, x=True, y=True, z=True):
        if x:
            for c in copies_x(e, depth):
                c.wait_send()
        if z:
            copy_z(e).wait_send()
        if y:
            up, down = copies_y(e)

            @pl.when(micro < 3)
            def _():
                up.wait_send()

            @pl.when(micro > 0)
            def _():
                down.wait_send()

    def pack_plane(packed, plane, i):
        for q in range(TILES):
            n = i * TILES + q
            tile = plane[8 * q : 8 * q + 8]
            packed = jnp.where(pack_id == n, pltpu.roll(tile, 2 * n, 1) if n else tile, packed)
        return packed

    def shifted_z(plane, message, i, step):
        tiles_up, tiles_down = [], []
        for q in range(TILES):
            n = i * TILES + q
            tile = plane[8 * q : 8 * q + 8]
            halo = pltpu.roll(message, NZ - 2 * n, 1) if n else message
            tiles_up.append(pltpu.roll(jnp.where(edge_up[step], halo, tile), NZ - step, 1))
            tiles_down.append(pltpu.roll(jnp.where(edge_down[step], halo, tile), step, 1))
        return jnp.concatenate(tiles_up, axis=0), jnp.concatenate(tiles_down, axis=0)

    def masked(plane, mask):
        return (plane.reshape(TILES, 8, NZ) * mask).reshape(NY, NZ)

    inner = pl.ds(8, NY)

    def put(e, i, plane):
        ex[e, 2 + i, inner, :] = plane

    def operator(e, write):
        message = zrecv[e]
        for i in range(NX):
            value = ex[e, 2 + i, inner, :]
            z_up, z_down = shifted_z(value, message, i, 2)
            total = coef[0, i] * value
            total -= coef[1, i] * ex[e, 4 + i, inner, :] + coef[2, i] * ex[e, i, inner, :]
            total -= coef[3, i] * ex[e, 2 + i, 10 : 10 + NY, :] + coef[4, i] * ex[e, 2 + i, 6 : 6 + NY, :]
            total -= coef[5, i] * z_up + coef[6, i] * z_down
            write(i, total)

    def red_copy(k, stage, step, peer, mine):
        n = stage * 8 + step
        return pltpu.make_async_remote_copy(
            src_ref=red.at[k, stage, mine], dst_ref=red.at[k, stage, mine],
            send_sem=red_send.at[k, n], recv_sem=red_recv.at[k, n], device_id=peer, device_id_type=MESH,
        )

    stages = ((peer_x, part_x, 8), (peer_y, part_y, 4), (peer_z, part_z, 4))

    def red_start(k, stage, rows):
        peer, mine, count = stages[stage]
        red[k, stage, mine] = rows
        for step in range(1, count):
            red_copy(k, stage, step, peer(step), mine).start()

    def red_finish(k, stage):
        peer, mine, count = stages[stage]
        for step in range(1, count):
            red_copy(k, stage, step, peer(step), mine).wait_recv()
        total = red[k, stage, 0]
        for j in range(1, count):
            total = total + red[k, stage, j]
        return total

    def red_drain(k):
        for stage, (peer, mine, count) in enumerate(stages):
            for step in range(1, count):
                red_copy(k, stage, step, peer(step), mine).wait_send()

    def partial_dots():
        sums = [None] * N_DOT
        for i in range(NX):
            r, w, p, s, t = r_[i], w_[i], p_[i], s_[i], t_[i]
            kp = s + SIGMA * p
            kr = w + SIGMA * r
            kkp = (t + SIGMA * s) + SIGMA * kp
            terms = (
                r * r, r * kp, r * kr, r * kkp, kp * kp, kp * kr, kp * kkp,
                kr * kr, kr * kkp, kkp * kkp, p * kp, p * kr, p * kkp,
            )
            for j, term in enumerate(terms):
                folded = term.reshape(TILES, 8, NZ).sum(axis=0)
                sums[j] = folded if i == 0 else sums[j] + folded
        rows = [jnp.sum(a, axis=0, keepdims=True) for a in sums]
        return jnp.concatenate(rows + [jnp.zeros((16 - N_DOT, NZ), F32)], axis=0)

    def scalars(rows):
        d = jnp.sum(rows, axis=1, keepdims=True)
        g = [d[j : j + 1, :] for j in range(N_DOT)]
        rr, rs, rw, rt, ss, sw, st, ww, wt, tt, ps, pw, pt = g
        alpha = rr / ps
        rr_1 = rr - 2.0 * alpha * rs + alpha * alpha * ss
        beta_1 = rr_1 / rr
        r_q = rw - alpha * rt + beta_1 * rs
        s_q = sw - alpha * st + beta_1 * ss
        p_q = pw - alpha * pt + beta_1 * ps
        alpha_1 = rr_1 / (r_q - alpha * s_q + beta_1 * p_q)
        w_q = ww - alpha * wt + beta_1 * sw
        t_q = wt - alpha * tt + beta_1 * st
        q_q = w_q - alpha * t_q + beta_1 * s_q
        rr_2 = rr_1 - 2.0 * alpha_1 * (r_q - alpha * s_q) + alpha_1 * alpha_1 * q_q
        beta_2 = rr_2 / rr_1
        return [jnp.broadcast_to(a, (NY, NZ)) for a in (alpha, beta_1, alpha_1, beta_2)]

    packed = jnp.zeros((8, NZ), F32)
    for i in range(NX):
        plane = disp_ref[i]
        put(E_DISP, i, plane)
        packed = pack_plane(packed, plane, i)
    zsend[E_DISP] = packed
    pl.semaphore_wait(barrier, len(friends))
    start(E_DISP, 1)
    prepare_weights(fin_ref, fmid_ref, fout_ref, ftan_ref, w_in, w_mid, w_out)
    finish(E_DISP, 1)
    message = zrecv[E_DISP]
    for i in range(NX):
        value = ex[E_DISP, 2 + i, inner, :]
        z_up, z_down = shifted_z(value, message, i, 1)
        strains = (
            (ex[E_DISP, 3 + i, inner, :] - ex[E_DISP, 1 + i, inner, :]) * 0.5,
            (ex[E_DISP, 2 + i, 9 : 9 + NY, :] - ex[E_DISP, 2 + i, 7 : 7 + NY, :]) * 0.5,
            (masked(z_up, keep_up_1) - masked(z_down, keep_down_1)) * 0.5,
        )
        rounded = [s.astype(BF16).astype(F32) for s in strains]
        family = lax.shift_right_logical(slot_ref[i], CAP_SHIFT).astype(F32)
        rows = rounded + [s - h for s, h in zip(strains, rounded)] + [family, flags_ref[i].astype(F32)]
        for k, row in enumerate(rows):
            points[pl.ds(i * NY * 8 + k, NY, stride=8), :] = row

    def chunk(j, carry):
        fibre_chunk(points, w_in, w_mid, w_out, pl.multiple_of(j * (8 * ROWS), 8 * ROWS))
        return carry

    lax.fori_loop(0, NX * NY // ROWS, chunk, 0)

    packed_t = packed_s = jnp.zeros((8, NZ), F32)
    for i in range(NX):
        sx, sy, sz, tan_high, tan_low = [points[pl.ds(i * NY * 8 + k, NY, stride=8), :] for k in range(5)]
        tangent = 0.5 + (tan_high + tan_low)
        put(E_SX, i, sx)
        put(E_SY, i, sy)
        put(E_TAN, i, tangent)
        s_z[i] = sz
        packed_s = pack_plane(packed_s, sz, i)
        packed_t = pack_plane(packed_t, tangent, i)
    zsend[E_SX] = packed_s
    zsend[E_TAN] = packed_t
    start(E_SX, 1, y=False)
    start(E_TAN, 1)
    start(E_SY, 1, x=False, z=False)
    finish(E_SX, 1, y=False)
    finish(E_TAN, 1)
    finish(E_SY, 1, x=False, z=False)
    message_s, message_t = zrecv[E_SX], zrecv[E_TAN]
    packed = jnp.zeros((8, NZ), F32)
    for i in range(NX):
        up, down = shifted_z(s_z[i], message_s, i, 1)
        total = (ex[E_SX, 3 + i, inner, :] - ex[E_SX, 1 + i, inner, :]) * 0.5
        total += (ex[E_SY, 2 + i, 9 : 9 + NY, :] - ex[E_SY, 2 + i, 7 : 7 + NY, :]) * 0.5
        total += (masked(up, keep_up_1) - masked(down, keep_down_1)) * 0.5
        rhs = load_ref[i] - found_ref[i] * disp_ref[i] + total
        put(E_R, i, rhs)
        packed = pack_plane(packed, rhs, i)
        r_[i] = rhs
        p_[i] = rhs
        x_[i] = jnp.zeros((NY, NZ), F32)
        u_[i] = jnp.zeros((NY, NZ), F32)
    zsend[E_R] = packed
    start(E_R, 2)
    for i in range(NX):
        up, down = shifted_z(ex[E_TAN, 2 + i, inner, :], message_t, i, 1)
        z_up, z_down = masked(up, keep_up_1) * 0.25, masked(down, keep_down_1) * 0.25
        x_up, x_down = ex[E_TAN, 3 + i, inner, :] * 0.25, ex[E_TAN, 1 + i, inner, :] * 0.25
        y_up, y_down = ex[E_TAN, 2 + i, 9 : 9 + NY, :] * 0.25, ex[E_TAN, 2 + i, 7 : 7 + NY, :] * 0.25
        coef[0, i] = found_ref[i] + ((x_up + x_down) + (y_up + y_down) + (z_up + z_down)) - SIGMA
        coef[1, i], coef[2, i] = x_up, x_down
        coef[3, i], coef[4, i] = y_up, y_down
        coef[5, i], coef[6, i] = masked(z_up, keep_up_2), masked(z_down, keep_down_2)

    class Packer:
        def __init__(self):
            self.packed = jnp.zeros((8, NZ), F32)

        def add(self, plane, i):
            self.packed = pack_plane(self.packed, plane, i)

    finish(E_R, 2)
    pack = Packer()

    def write_w(i, value):
        put(E_W, i, value)
        w_[i] = value
        s_[i] = value
        pack.add(value, i)

    operator(E_R, write_w)
    zsend[E_W] = pack.packed
    start(E_W, 2)
    finish(E_W, 2)
    pack_t = Packer()

    def write_z(i, value):
        put(E_T, i, value)
        z_[i] = value
        t_[i] = value
        pack_t.add(value, i)

    operator(E_W, write_z)
    zsend[E_T] = pack_t.packed

    def block(k, beta):
        e_t, e_u = E_T + 2 * k, E_T + 2 * k + 1
        start(e_t, 2)
        red_start(k, 0, partial_dots())
        finish(e_t, 2)
        pack_u = Packer()

        def write_u(i, value):
            put(e_u, i, value)
            z2_[i] = value - beta * u_[i]
            u_[i] = value
            pack_u.add(value, i)

        operator(e_t, write_u)
        zsend[e_u] = pack_u.packed
        start(e_u, 2)
        red_start(k, 1, red_finish(k, 0))
        red_start(k, 2, red_finish(k, 1))
        finish(e_u, 2)

        def write_v(i, value):
            v_[i] = value

        operator(e_u, write_v)
        alpha, beta_1, alpha_1, beta_2 = scalars(red_finish(k, 2))
        pack_n = Packer()
        tangents = []
        for i in range(NX):
            p, s, t, u = p_[i], s_[i], t_[i], u_[i]
            x = x_[i] + alpha * p
            r = r_[i] - alpha * (s + SIGMA * p)
            w = w_[i] - alpha * (t + SIGMA * s)
            z = z_[i] - alpha * (u + SIGMA * t)
            z2 = z2_[i] - alpha * (v_[i] + SIGMA * u)
            p = r + beta_1 * p
            s = w + beta_1 * s
            t = z + beta_1 * t
            u = z2 + beta_1 * u
            x_[i] = x + alpha_1 * p
            r = r - alpha_1 * (s + SIGMA * p)
            w = w - alpha_1 * (t + SIGMA * s)
            z = z - alpha_1 * (u + SIGMA * t)
            r_[i], w_[i], z_[i], u_[i] = r, w, z, u
            p_[i] = r + beta_2 * p
            s_[i] = w + beta_2 * s
            t = z + beta_2 * t
            t_[i] = t
            tangents.append(t)
        for i in range(NX):
            pack_n.add(tangents[i], i)

        @pl.when(k < 2)
        def _():
            for i in range(NX):
                put(e_t + 2, i, tangents[i])
            zsend[e_t + 2] = pack_n.packed

        return beta_2

    lax.fori_loop(0, 3, block, jnp.zeros((NY, NZ), F32))

    last = N_RED - 1
    red_start(last, 0, partial_dots())
    red_start(last, 1, red_finish(last, 0))
    red_start(last, 2, red_finish(last, 1))
    alpha, beta_1, alpha_1, _ = scalars(red_finish(last, 2))
    for i in range(NX):
        p, s, t = p_[i], s_[i], t_[i]
        x = x_[i] + alpha * p
        r = r_[i] - alpha * (s + SIGMA * p)
        w = w_[i] - alpha * (t + SIGMA * s)
        p = r + beta_1 * p
        s = w + beta_1 * s
        field_out[i] = disp_ref[i] + (x + alpha_1 * p)
        residual_out[i] = r - alpha_1 * (s + SIGMA * p)

    drain(E_DISP, 1)
    drain(E_SX, 1, y=False)
    drain(E_TAN, 1)
    drain(E_SY, 1, x=False, z=False)

    def drain_step(e, carry):
        drain(e, 2)
        return carry

    lax.fori_loop(E_R, N_EX, drain_step, 0)

    def drain_red(k, carry):
        red_drain(k)
        return carry

    lax.fori_loop(0, N_RED, drain_red, 0)


def body(*args):
    shape = (NX, NY, NZ)
    field = pltpu.VMEM(shape, F32)
    whole = pl.BlockSpec(memory_space=pltpu.VMEM)
    return pl.pallas_call(
        newton_kernel,
        out_shape=(jax.ShapeDtypeStruct(shape, F32), jax.ShapeDtypeStruct(shape, F32)),
        in_specs=[whole] * 9,
        out_specs=(whole, whole),
        scratch_shapes=[
            pltpu.VMEM((N_EX, NX + 4, NY + 16, NZ), F32),
            pltpu.VMEM((N_EX, 8, NZ), F32),
            pltpu.VMEM((N_EX, 8, NZ), F32),
            pltpu.VMEM((N_RED, 3, 8, 16, NZ), F32),
            pltpu.VMEM((NX * NY * 8, NZ), F32),
            pltpu.VMEM((MODES, 64), BF16),
            pltpu.VMEM((MODES, FAMILIES * MODES), BF16),
            pltpu.VMEM((32, 2 * MODES), BF16),
            pltpu.VMEM((7,) + shape, F32),
            field,
        ]
        + [field] * 10
        + [
            pltpu.SemaphoreType.DMA((N_EX, 5)),
            pltpu.SemaphoreType.DMA((N_EX, 5)),
            pltpu.SemaphoreType.DMA((N_RED, 24)),
            pltpu.SemaphoreType.DMA((N_RED, 24)),
        ],
        compiler_params=pltpu.CompilerParams(
            collective_id=0, has_side_effects=True, vmem_limit_bytes=60 * 1024 * 1024
        ),
        name="newton_step",
    )(*args)


def solution(mesh):
    placed = P("blk", "micro", "slab")
    return jax.shard_map(
        body,
        mesh=mesh,
        in_specs=(placed,) * 5 + (P(),) * 4,
        out_specs=(placed, placed),
        check_vma=False,
    )
```

time: 1550 us -> 113 us (0.07)
  blocking collectives: 953 us -> 0 us
  local copies, waits for them, and re-layouts: 272 us -> 4.18 us
  starting transfers between devices: 122 us -> 0 us
  Pallas kernels: 0 us -> 108 us
  matrix products: 72.6 us -> 0 us
  waiting for transfers between devices: 69.2 us -> 0 us
  other arithmetic: 22.7 us -> 0 us
  between operations: 22 us -> 0.66 us
    psum x15 -> x0, blocking collectives: 953 us -> none  [global_sum(): return lax.psum(value, ('blk', 'slab', 'micro'))]
    ppermute x60 -> x0, starting transfers between devices: 122 us -> none  [the longest x30 73 us: padded_2(): lax.ppermute(tail, axis, [(i, (i + 1) % count) for i in range(ends)])]
    gather x1 -> x0, local copies, waits for them, and re-layouts: 119 us -> none  [body(): returned.reshape(4, family_count * capacity)[:, slots]]
    pallas_call x0 -> x1, Pallas kernels: none -> 108 us  [body(): pl.pallas_call(newton_kernel, out_shape=(jax.ShapeDtypeStruct(shape, F32)...]
    scatter x1 -> x0, local copies, waits for them, and re-layouts: 93.5 us -> none  [body(): padded = jnp.zeros((4, family_count * capacity), jnp.float32).at[:, slots...]
    dot_general x12 -> x0, matrix products: 72.6 us -> none  [the longest x4 37.9 us: fibre_model(): jnp.dot(weight_tan, widened * widened, precision=lax.Precision.HIGHEST)]
    ppermute x60 -> x0, waiting for transfers between devices: 69.2 us -> none  [the longest x30 47.2 us: padded_2(): lax.ppermute(head, axis, [((i + 1) % count, i) for i in range(ends)])]
    reshape x2 -> x0, local copies, waits for them, and re-layouts: 28.1 us -> none  [the longest x1 18.1 us: body(): padded = jnp.zeros((4, family_count * capacity), jnp.float32).at[:, slots...]
  transfers between devices with their start and end apart: 60 -> 0, of which waited for: 20 -> 0; matrix products, arithmetic and copies ran while one was open for 1% -> 0% of each run, Pallas kernels for 0% -> 0%
where the time goes in v1:
time: 113 us
  Pallas kernels  108 us (96%)
  local copies, waits for them, and re-layouts  4.18 us (4%)
    pallas_call x1, Pallas kernels, body(): pl.pallas_call(newton_kernel, out_shape=(jax.ShapeDtypeStruct(shape, F32)...  108 us
    unnamed x8, local copies, waits for them, and re-layouts  4.18 us

profile of v1, /device:TPU:0, one launch (start us, length us, event | category | flops | bytes accessed | tf_op | source)
XLA Modules:
  0.0 113.2 jit_solution(14072987704353017981)
XLA Ops:
  0.6 0.0 copy-start.1
  0.6 1.3 %copy.12.fout_ref = bf16[4,3,256]{2,1,0:T(4,128)(2,1)} copy(bf16[4,3,256]{2,0,1:T(4,128)(2,1)} %param.16) | data formatting | bytes 12288 | tf_op args[7]
  1.9 0.0 copy-done.1
  1.9 0.6 copy.11.fin_ref
  2.6 108.4 %newton_step.1 = (f32[8,32,128]{2,1,0:T(8,128)}, f32[8,32,128]{2,1,0:T(8,128)}) custom-call(f32[8,32,128]{2,1,0:T(8,128)} %disp_ref.1, f32[8,32,128]{2,1,0:T(8,128)} %load_ref.1, f32[8,32,128]{2,1,0:T(8,128)} %found_ref.1, s32[8,32,128]{2,1,0:T(8,128)} %flags_ref.1, s32[8,32,128]{2,1,0:T(8,128)} %slot_ref.1, f32[4,3,256]{2,1,0:T(4,128)} %copy.11.fin_ref, ...), custom_call_target="tpu_custom_call" | custom-call | tf_op jit(solution)/shard_map/newton_step/pallas_call | solution.py:510
  110.9 0.0 copy-start
  110.9 1.6 %copy.15 = f32[8,32,128]{2,1,0:T(8,128)} copy(f32[8,32,128]{2,1,0:T(8,128)} %get-tuple-element.4) | data formatting | bytes 262144
  112.5 0.0 copy-done
  112.6 0.7 copy.16
Async XLA Ops:
  0.6 1.3 %copy-start.1 = (f32[4,3,256]{2,0,1:T(4,128)S(1)}, f32[4,3,256]{2,0,1:T(4,128)}, u32[]{:S(2)}) copy-start(f32[4,3,256]{2,0,1:T(4,128)} %param.14) | copy-start | bytes 36868
  110.9 1.6 %copy-start = (f32[8,32,128]{2,1,0:T(8,128)S(1)}, f32[8,32,128]{2,1,0:T(8,128)}, u32[]{:S(2)}) copy-start(f32[8,32,128]{2,1,0:T(8,128)} %get-tuple-element.5) | copy-start | bytes 393220

commit v2 on v1

--- a/solution.py
+++ b/solution.py
@@ -11,37 +11,38 @@
 FAMILIES = 4
 MODES = 256
 CAP_SHIFT = 14
-ROWS = 16
 SIGMA = 3.0
 NX, NY, NZ = 8, 32, 128
 TILES = NY // 8
 E_DISP, E_TAN, E_SX, E_SY, E_R, E_W, E_T = 0, 1, 2, 3, 4, 5, 6
 N_EX = 12
 N_RED = 4
+N_IN = 12
+FIX = NX * NY * 8
 N_DOT = 13
 
 
-def prepare_weights(family_in, family_mid, family_out, family_tan, w_in, w_mid, w_out):
+def prepare_weights(family_in, family_out, family_tan, w_in, w_out):
     zero = jnp.zeros((1, MODES), F32)
     high, low, stress, tangent = [], [], [], []
     for f in range(FAMILIES):
-        weight = family_in[f]
+        weight = family_in[:, f, :]
         rounded = weight.astype(BF16).astype(F32)
         high += [rounded, rounded, zero, zero]
         low += [weight - rounded, zero, zero, zero, zero, zero]
-        w_mid[:, f * MODES : (f + 1) * MODES] = family_mid[f]
         tan = family_tan[f : f + 1, :]
         tan_high = tan.astype(BF16).astype(F32)
-        stress += [family_out[f].astype(F32)] + [zero] * 5
+        stress += [family_out[:, f, :].astype(F32)] + [zero] * 5
         tangent += [zero] * 3 + [tan_high, tan - tan_high] + [zero] * 3
     w_in[...] = jnp.concatenate(high + low, axis=0).T.astype(BF16)
     w_out[:, :MODES] = jnp.concatenate(stress, axis=0).astype(BF16)
     w_out[:, MODES:] = jnp.concatenate(tangent, axis=0).astype(BF16)
 
 
-def fibre_chunk(points, w_in, w_mid, w_out, base):
-    width = ROWS * NZ
-    rows = jnp.concatenate([points[pl.ds(base + 8 * i, 8), :] for i in range(ROWS)], axis=1)
+def fibre_chunk(points, w_in, w_mid, w_out, bases):
+    places = [base + 8 * i for base in bases for i in range(8)]
+    width = len(places) * NZ
+    rows = jnp.concatenate([points[pl.ds(place, 8), :] for place in places], axis=1)
     family, flag = rows[6:7, :], rows[7:8, :]
     family_8 = jnp.broadcast_to(family, (8, width))
     chosen = [family_8 == float(f) for f in range(FAMILIES)]
@@ -64,42 +65,48 @@
     picked = jnp.where(
         chosen[0], out[0:8], jnp.where(chosen[1], out[8:16], jnp.where(chosen[2], out[16:24], out[24:32]))
     )
-    for i in range(ROWS):
-        points[pl.ds(base + 8 * i, 8), :] = picked[:, i * NZ : (i + 1) * NZ]
+    for i, place in enumerate(places):
+        points[pl.ds(place, 8), :] = picked[:, i * NZ : (i + 1) * NZ]
 
 
 def newton_kernel(
-    disp_ref, load_ref, found_ref, flags_ref, slot_ref, fin_ref, fmid_ref, fout_ref, ftan_ref,
+    disp_hbm, load_hbm, found_hbm, flags_hbm, slot_hbm, fin_hbm, fmid_hbm, fout_hbm, ftan_hbm,
     field_out, residual_out,
+    load_ref, found_ref, flags_ref, slot_ref, fin_ref, fout_ref, ftan_ref,
     ex, zsend, zrecv, red, points, w_in, w_mid, w_out, coef, s_z,
     x_, r_, w_, z_, z2_, p_, s_, t_, u_, v_,
-    send_sem, recv_sem, red_send, red_recv,
+    send_sem, recv_sem, red_send, red_recv, in_sem,
 ):
+    inner = pl.ds(8, NY)
+    pairs = [(disp_hbm, ex.at[E_DISP, pl.ds(2, NX), inner, :]), (slot_hbm, slot_ref), (flags_hbm, flags_ref)]
+    pairs += [(fin_hbm, fin_ref), (fout_hbm, fout_ref), (ftan_hbm, ftan_ref)]
+    pairs += [(fmid_hbm.at[f], w_mid.at[:, pl.ds(f * MODES, MODES)]) for f in range(FAMILIES)]
+    pairs += [(found_hbm, found_ref), (load_hbm, load_ref)]
+    loads = [pltpu.make_async_copy(a, b, in_sem.at[j]) for j, (a, b) in enumerate(pairs)]
+    for c in loads:
+        c.start()
     blk, slab, micro = lax.axis_index("blk"), lax.axis_index("slab"), lax.axis_index("micro")
     n_blk = lax.axis_size("blk")
     up_blk, down_blk = lax.rem(blk + 1, n_blk), lax.rem(blk + n_blk - 1, n_blk)
     part_x = slab * 4 + micro
-    part_y, part_z = lax.rem(blk, 4), lax.div(blk, 4)
 
     def peer_x(step):
         other = lax.rem(part_x + step, 8)
         return (blk, lax.div(other, 4), lax.rem(other, 4))
 
-    def peer_y(step):
-        return (part_z * 4 + lax.rem(part_y + step, 4), slab, micro)
-
-    def peer_z(step):
-        return (lax.rem(part_z + step, 4) * 4 + part_y, slab, micro)
+    def peer_blk(step):
+        return (lax.rem(blk + step, n_blk), slab, micro)
 
     barrier = pltpu.get_barrier_semaphore()
-    friends = [peer_x(j) for j in range(1, 8)] + [peer_y(j) for j in range(1, 4)]
-    friends += [peer_z(j) for j in range(1, 4)] + [(up_blk, slab, micro), (down_blk, slab, micro)]
+    friends = [peer_x(j) for j in range(1, 8)] + [peer_blk(j) for j in range(1, 16)]
     for friend in friends:
         pl.semaphore_signal(barrier, inc=1, device_id=friend, device_id_type=MESH)
 
     lane = lax.broadcasted_iota(jnp.int32, (8, NZ), 1)
+    diagonal = lax.broadcasted_iota(jnp.int32, (16, NZ), 0) == lax.broadcasted_iota(jnp.int32, (16, NZ), 1)
     first_slab, last_slab = slab == 0, slab == 1
-    pack_id = lax.shift_right_logical(lax.rem(lane + 2 * (1 - slab), NZ), 1)
+    pack_id = {n: lax.div(lax.rem(lane + n * (1 - slab), NZ), n) for n in (1, 2)}
+    edge_own = jnp.logical_or(jnp.logical_and(lane == NZ - 1, slab == 0), jnp.logical_and(lane == 0, slab == 1))
     edge_up = {n: jnp.logical_and(lane < n, first_slab) for n in (1, 2)}
     edge_down = {n: jnp.logical_and(lane >= NZ - n, last_slab) for n in (1, 2)}
 
@@ -203,11 +210,11 @@
             def _():
                 down.wait_send()
 
-    def pack_plane(packed, plane, i):
+    def pack_plane(packed, plane, i, step=2):
         for q in range(TILES):
             n = i * TILES + q
             tile = plane[8 * q : 8 * q + 8]
-            packed = jnp.where(pack_id == n, pltpu.roll(tile, 2 * n, 1) if n else tile, packed)
+            packed = jnp.where(pack_id[step] == n, pltpu.roll(tile, step * n, 1) if n else tile, packed)
         return packed
 
     def shifted_z(plane, message, i, step):
@@ -215,15 +222,13 @@
         for q in range(TILES):
             n = i * TILES + q
             tile = plane[8 * q : 8 * q + 8]
-            halo = pltpu.roll(message, NZ - 2 * n, 1) if n else message
+            halo = pltpu.roll(message, NZ - step * n, 1) if n else message
             tiles_up.append(pltpu.roll(jnp.where(edge_up[step], halo, tile), NZ - step, 1))
             tiles_down.append(pltpu.roll(jnp.where(edge_down[step], halo, tile), step, 1))
         return jnp.concatenate(tiles_up, axis=0), jnp.concatenate(tiles_down, axis=0)
 
     def masked(plane, mask):
-        return (plane.reshape(TILES, 8, NZ) * mask).reshape(NY, NZ)
-
-    inner = pl.ds(8, NY)
+        return (plane.reshape(-1, 8, NZ) * mask).reshape(plane.shape)
 
     def put(e, i, plane):
         ex[e, 2 + i, inner, :] = plane
@@ -240,13 +245,13 @@
             write(i, total)
 
     def red_copy(k, stage, step, peer, mine):
-        n = stage * 8 + step
+        n = stage * 16 + step
         return pltpu.make_async_remote_copy(
             src_ref=red.at[k, stage, mine], dst_ref=red.at[k, stage, mine],
             send_sem=red_send.at[k, n], recv_sem=red_recv.at[k, n], device_id=peer, device_id_type=MESH,
         )
 
-    stages = ((peer_x, part_x, 8), (peer_y, part_y, 4), (peer_z, part_z, 4))
+    stages = ((peer_x, part_x, 8), (peer_blk, blk, 16))
 
     def red_start(k, stage, rows):
         peer, mine, count = stages[stage]
@@ -283,10 +288,12 @@
                 folded = term.reshape(TILES, 8, NZ).sum(axis=0)
                 sums[j] = folded if i == 0 else sums[j] + folded
         rows = [jnp.sum(a, axis=0, keepdims=True) for a in sums]
-        return jnp.concatenate(rows + [jnp.zeros((16 - N_DOT, NZ), F32)], axis=0)
+        rows = jnp.concatenate(rows + [jnp.zeros((16 - N_DOT, NZ), F32)], axis=0)
+        sums = jnp.broadcast_to(jnp.sum(rows, axis=1, keepdims=True), (16, NZ))
+        return jnp.sum(jnp.where(diagonal, sums, 0.0), axis=0, keepdims=True)
 
     def scalars(rows):
-        d = jnp.sum(rows, axis=1, keepdims=True)
+        d = jnp.sum(jnp.where(diagonal, jnp.broadcast_to(rows, (16, NZ)), 0.0), axis=1, keepdims=True)
         g = [d[j : j + 1, :] for j in range(N_DOT)]
         rr, rs, rw, rt, ss, sw, st, ww, wt, tt, ps, pw, pt = g
         alpha = rr / ps
@@ -303,52 +310,112 @@
         beta_2 = rr_2 / rr_1
         return [jnp.broadcast_to(a, (NY, NZ)) for a in (alpha, beta_1, alpha_1, beta_2)]
 
-    packed = jnp.zeros((8, NZ), F32)
+    zeros = jnp.zeros((8, NZ), F32)
+
+    def strains_at(i, top, count, halo):
+        rows = pl.ds(8 + top, count)
+        value = ex[E_DISP, 2 + i, rows, :]
+        if halo is None:
+            z_up, z_down = pltpu.roll(value, NZ - 1, 1), pltpu.roll(value, 1, 1)
+        else:
+            z_up, z_down = shifted_z(value, halo, i, 1)
+        z_up, z_down = masked(z_up, keep_up_1), masked(z_down, keep_down_1)
+        return (
+            (ex[E_DISP, 3 + i, rows, :] - ex[E_DISP, 1 + i, rows, :]) * 0.5,
+            (ex[E_DISP, 2 + i, 9 + top : 9 + top + count, :] - ex[E_DISP, 2 + i, 7 + top : 7 + top + count, :]) * 0.5,
+            (z_up - z_down) * 0.5,
+        )
+
+    def store_points(base, count, strains, family, flag):
+        rounded = [s.astype(BF16).astype(F32) for s in strains]
+        rows = rounded + [s - h for s, h in zip(strains, rounded)] + [family, flag]
+        for k, row in enumerate(rows):
+            points[pl.ds(base + k, count, stride=8), :] = row
+
+    def traits(i, top, count):
+        family = lax.shift_right_logical(slot_ref[i, top : top + count, :], CAP_SHIFT).astype(F32)
+        return family, flags_ref[i, top : top + count, :].astype(F32)
+
+    def chunks(first, last, place):
+        def chunk(j, carry):
+            fibre_chunk(points, w_in, w_mid, w_out, [pl.multiple_of(base, 64) for base in place(j)])
+            return carry
+
+        lax.fori_loop(first, last, chunk, 0)
+
+    middle = range(1, NX - 1)
+    loads[0].wait()
+    packed = zeros
     for i in range(NX):
-        plane = disp_ref[i]
-        put(E_DISP, i, plane)
-        packed = pack_plane(packed, plane, i)
+        packed = pack_plane(packed, ex[E_DISP, 2 + i, inner, :], i, 1)
     zsend[E_DISP] = packed
+    for c in loads[1:10]:
+        c.wait()
+    prepare_weights(fin_ref, fout_ref, ftan_ref, w_in, w_out)
+    for i in middle:
+        store_points((i * NY + 8) * 8, 16, strains_at(i, 8, 16, None), *traits(i, 8, 16))
     pl.semaphore_wait(barrier, len(friends))
     start(E_DISP, 1)
-    prepare_weights(fin_ref, fmid_ref, fout_ref, ftan_ref, w_in, w_mid, w_out)
+
+    def middle_rows(j):
+        return j * (NY * 8) + 64, j * (NY * 8) + 128
+
+    chunks(1, 4, middle_rows)
     finish(E_DISP, 1)
     message = zrecv[E_DISP]
+    edges = [zeros] * 5
     for i in range(NX):
-        value = ex[E_DISP, 2 + i, inner, :]
-        z_up, z_down = shifted_z(value, message, i, 1)
-        strains = (
-            (ex[E_DISP, 3 + i, inner, :] - ex[E_DISP, 1 + i, inner, :]) * 0.5,
-            (ex[E_DISP, 2 + i, 9 : 9 + NY, :] - ex[E_DISP, 2 + i, 7 : 7 + NY, :]) * 0.5,
-            (masked(z_up, keep_up_1) - masked(z_down, keep_down_1)) * 0.5,
-        )
-        rounded = [s.astype(BF16).astype(F32) for s in strains]
-        family = lax.shift_right_logical(slot_ref[i], CAP_SHIFT).astype(F32)
-        rows = rounded + [s - h for s, h in zip(strains, rounded)] + [family, flags_ref[i].astype(F32)]
-        for k, row in enumerate(rows):
-            points[pl.ds(i * NY * 8 + k, NY, stride=8), :] = row
-
-    def chunk(j, carry):
-        fibre_chunk(points, w_in, w_mid, w_out, pl.multiple_of(j * (8 * ROWS), 8 * ROWS))
-        return carry
-
-    lax.fori_loop(0, NX * NY // ROWS, chunk, 0)
-
-    packed_t = packed_s = jnp.zeros((8, NZ), F32)
+        strains = strains_at(i, 0, NY, message)
+        family, flag = traits(i, 0, NY)
+        columns = strains + (family, flag)
+        edges = [pack_plane(e, c, i, 1) for e, c in zip(edges, columns)]
+        for top in (0, 8, 16, 24):
+            if i in (0, NX - 1) or top in (0, 24):
+                part = [c[top : top + 8] for c in columns]
+                store_points((i * NY + top) * 8, 8, part[:3], part[3], part[4])
+    store_points(FIX, 8, edges[:3], edges[3], edges[4])
+    fibre_chunk(points, w_in, w_mid, w_out, [FIX])
+
+    def face_rows(j):
+        base = lax.div(j, 2) * ((NX - 1) * NY * 8) + lax.rem(j, 2) * 128
+        return base, base + 64
+
+    def side_rows(j):
+        return j * (NY * 8), j * (NY * 8) + 192
+
+    chunks(0, 4, face_rows)
+    chunks(1, NX - 1, side_rows)
+
+    def results(base, count):
+        sx, sy, sz, high, low = [points[pl.ds(base + k, count, stride=8), :] for k in range(5)]
+        return sx, sy, sz, 0.5 + (high + low)
+
+    def keep_results(i, top, count, values):
+        rows = pl.ds(8 + top, count)
+        ex[E_SX, 2 + i, rows, :] = values[0]
+        ex[E_SY, 2 + i, rows, :] = values[1]
+        s_z[i, pl.ds(top, count), :] = values[2]
+        ex[E_TAN, 2 + i, rows, :] = values[3]
+
+    edges = results(FIX, 8)
+    zsend[E_SX] = edges[2]
+    zsend[E_TAN] = edges[3]
     for i in range(NX):
-        sx, sy, sz, tan_high, tan_low = [points[pl.ds(i * NY * 8 + k, NY, stride=8), :] for k in range(5)]
-        tangent = 0.5 + (tan_high + tan_low)
-        put(E_SX, i, sx)
-        put(E_SY, i, sy)
-        put(E_TAN, i, tangent)
-        s_z[i] = sz
-        packed_s = pack_plane(packed_s, sz, i)
-        packed_t = pack_plane(packed_t, tangent, i)
-    zsend[E_SX] = packed_s
-    zsend[E_TAN] = packed_t
+        for top, count in ((0, NY),) if i in (0, NX - 1) else ((0, 8), (24, 8)):
+            keep_results(i, top, count, results((i * NY + top) * 8, count))
     start(E_SX, 1, y=False)
     start(E_TAN, 1)
     start(E_SY, 1, x=False, z=False)
+    chunks(4, NX - 1, middle_rows)
+    for i in middle:
+        for top in (8, 16):
+            n = i * TILES + top // 8
+            values = results((i * NY + top) * 8, 8)
+            values = [jnp.where(edge_own, pltpu.roll(e, NZ - n, 1), v) for e, v in zip(edges, values)]
+            keep_results(i, top, 8, values)
+
+    loads[10].wait()
+    loads[11].wait()
     finish(E_SX, 1, y=False)
     finish(E_TAN, 1)
     finish(E_SY, 1, x=False, z=False)
@@ -359,7 +426,7 @@
         total = (ex[E_SX, 3 + i, inner, :] - ex[E_SX, 1 + i, inner, :]) * 0.5
         total += (ex[E_SY, 2 + i, 9 : 9 + NY, :] - ex[E_SY, 2 + i, 7 : 7 + NY, :]) * 0.5
         total += (masked(up, keep_up_1) - masked(down, keep_down_1)) * 0.5
-        rhs = load_ref[i] - found_ref[i] * disp_ref[i] + total
+        rhs = load_ref[i] - found_ref[i] * ex[E_DISP, 2 + i, inner, :] + total
         put(E_R, i, rhs)
         packed = pack_plane(packed, rhs, i)
         r_[i] = rhs
@@ -413,6 +480,7 @@
         e_t, e_u = E_T + 2 * k, E_T + 2 * k + 1
         start(e_t, 2)
         red_start(k, 0, partial_dots())
+        red_start(k, 1, red_finish(k, 0))
         finish(e_t, 2)
         pack_u = Packer()
 
@@ -425,15 +493,13 @@
         operator(e_t, write_u)
         zsend[e_u] = pack_u.packed
         start(e_u, 2)
-        red_start(k, 1, red_finish(k, 0))
-        red_start(k, 2, red_finish(k, 1))
         finish(e_u, 2)
 
         def write_v(i, value):
             v_[i] = value
 
         operator(e_u, write_v)
-        alpha, beta_1, alpha_1, beta_2 = scalars(red_finish(k, 2))
+        alpha, beta_1, alpha_1, beta_2 = scalars(red_finish(k, 1))
         pack_n = Packer()
         tangents = []
         for i in range(NX):
@@ -473,8 +539,7 @@
     last = N_RED - 1
     red_start(last, 0, partial_dots())
     red_start(last, 1, red_finish(last, 0))
-    red_start(last, 2, red_finish(last, 1))
-    alpha, beta_1, alpha_1, _ = scalars(red_finish(last, 2))
+    alpha, beta_1, alpha_1, _ = scalars(red_finish(last, 1))
     for i in range(NX):
         p, s, t = p_[i], s_[i], t_[i]
         x = x_[i] + alpha * p
@@ -482,7 +547,7 @@
         w = w_[i] - alpha * (t + SIGMA * s)
         p = r + beta_1 * p
         s = w + beta_1 * s
-        field_out[i] = disp_ref[i] + (x + alpha_1 * p)
+        field_out[i] = ex[E_DISP, 2 + i, inner, :] + (x + alpha_1 * p)
         residual_out[i] = r - alpha_1 * (s + SIGMA * p)
 
     drain(E_DISP, 1)
@@ -503,21 +568,30 @@
     lax.fori_loop(0, N_RED, drain_red, 0)
 
 
-def body(*args):
+def body(displacement, load_field, foundation, flags, slots, family_in, family_mid, family_out, family_tan):
+    family_in, family_out = jnp.transpose(family_in, (1, 0, 2)), jnp.transpose(family_out, (1, 0, 2))
     shape = (NX, NY, NZ)
     field = pltpu.VMEM(shape, F32)
+    ints = pltpu.VMEM(shape, jnp.int32)
     whole = pl.BlockSpec(memory_space=pltpu.VMEM)
     return pl.pallas_call(
         newton_kernel,
         out_shape=(jax.ShapeDtypeStruct(shape, F32), jax.ShapeDtypeStruct(shape, F32)),
-        in_specs=[whole] * 9,
+        in_specs=[pl.BlockSpec(memory_space=pl.ANY)] * 9,
         out_specs=(whole, whole),
         scratch_shapes=[
+            field,
+            field,
+            ints,
+            ints,
+            pltpu.VMEM((3, FAMILIES, MODES), F32),
+            pltpu.VMEM((3, FAMILIES, MODES), BF16),
+            pltpu.VMEM((FAMILIES, MODES), F32),
             pltpu.VMEM((N_EX, NX + 4, NY + 16, NZ), F32),
             pltpu.VMEM((N_EX, 8, NZ), F32),
             pltpu.VMEM((N_EX, 8, NZ), F32),
-            pltpu.VMEM((N_RED, 3, 8, 16, NZ), F32),
-            pltpu.VMEM((NX * NY * 8, NZ), F32),
+            pltpu.VMEM((N_RED, 2, 16, 1, NZ), F32),
+            pltpu.VMEM((FIX + 64, NZ), F32),
             pltpu.VMEM((MODES, 64), BF16),
             pltpu.VMEM((MODES, FAMILIES * MODES), BF16),
             pltpu.VMEM((32, 2 * MODES), BF16),
@@ -528,14 +602,15 @@
         + [
             pltpu.SemaphoreType.DMA((N_EX, 5)),
             pltpu.SemaphoreType.DMA((N_EX, 5)),
-            pltpu.SemaphoreType.DMA((N_RED, 24)),
-            pltpu.SemaphoreType.DMA((N_RED, 24)),
+            pltpu.SemaphoreType.DMA((N_RED, 32)),
+            pltpu.SemaphoreType.DMA((N_RED, 32)),
+            pltpu.SemaphoreType.DMA((N_IN,)),
         ],
         compiler_params=pltpu.CompilerParams(
             collective_id=0, has_side_effects=True, vmem_limit_bytes=60 * 1024 * 1024
         ),
         name="newton_step",
-    )(*args)
+    )(displacement, load_field, foundation, flags, slots, family_in, family_mid, family_out, family_tan)
 
 
 def solution(mesh):

time: 113 us -> 94 us (0.83)
  Pallas kernels: 108 us -> 90.9 us
  local copies, waits for them, and re-layouts: 4.18 us -> 2.26 us
    pallas_call x1, Pallas kernels: 108 us -> 90.9 us  [body(): pl.pallas_call(newton_kernel, out_shape=(jax.ShapeDtypeStruct(shape, F32)...]
    unnamed x8 -> x4, local copies, waits for them, and re-layouts: 4.18 us -> 2.26 us
where the time goes in v2:
time: 94 us; the launch traced here: 93.8 us
  Pallas kernels  90.9 us (97%)
  local copies, waits for them, and re-layouts  2.26 us (2%)
    pallas_call x1, Pallas kernels, body(): pl.pallas_call(newton_kernel, out_shape=(jax.ShapeDtypeStruct(shape, F32)...  90.9 us
    unnamed x4, local copies, waits for them, and re-layouts  2.26 us

profile of v2, /device:TPU:0, one launch (start us, length us, event | category | flops | bytes accessed | tf_op | source)
XLA Modules:
  0.0 93.8 jit_solution(8985035784010393846)
XLA Ops:
  0.6 90.9 %newton_step.1 = (f32[8,32,128]{2,1,0:T(8,128)}, f32[8,32,128]{2,1,0:T(8,128)}) custom-call(f32[8,32,128]{2,1,0:T(8,128)} %disp_hbm.1, f32[8,32,128]{2,1,0:T(8,128)} %load_hbm.1, f32[8,32,128]{2,1,0:T(8,128)} %found_hbm.1, s32[8,32,128]{2,1,0:T(8,128)} %flags_hbm.1, s32[8,32,128]{2,1,0:T(8,128)} %slot_hbm.1, f32[3,4,256]{2,1,0:T(4,128)} %bitcast.2, ...), custom_call_target="tpu_custom_call" | custom-call | tf_op jit(solution)/shard_map/newton_step/pallas_call | solution.py:577
  91.5 0.0 copy-start
  91.5 1.6 %copy.13 = f32[8,32,128]{2,1,0:T(8,128)} copy(f32[8,32,128]{2,1,0:T(8,128)} %get-tuple-element.4) | data formatting | bytes 262144
  93.1 0.0 copy-done
  93.1 0.7 copy.14
Async XLA Ops:
  91.5 1.6 %copy-start = (f32[8,32,128]{2,1,0:T(8,128)S(1)}, f32[8,32,128]{2,1,0:T(8,128)}, u32[]{:S(2)}) copy-start(f32[8,32,128]{2,1,0:T(8,128)} %get-tuple-element.5) | copy-start | bytes 393220

commit v3 on v2

--- a/solution.py
+++ b/solution.py
@@ -16,6 +16,8 @@
 TILES = NY // 8
 E_DISP, E_TAN, E_SX, E_SY, E_R, E_W, E_T = 0, 1, 2, 3, 4, 5, 6
 N_EX = 12
+INSIDE = (2, 3, 4, 5)
+OUTSIDE = (0, 1, 6, 7)
 N_RED = 4
 N_IN = 12
 FIX = NX * NY * 8
@@ -71,7 +73,7 @@
 
 def newton_kernel(
     disp_hbm, load_hbm, found_hbm, flags_hbm, slot_hbm, fin_hbm, fmid_hbm, fout_hbm, ftan_hbm,
-    field_out, residual_out,
+    gain_out, residual_out, change_out,
     load_ref, found_ref, flags_ref, slot_ref, fin_ref, fout_ref, ftan_ref,
     ex, zsend, zrecv, red, points, w_in, w_mid, w_out, coef, s_z,
     x_, r_, w_, z_, z2_, p_, s_, t_, u_, v_,
@@ -233,9 +235,9 @@
     def put(e, i, plane):
         ex[e, 2 + i, inner, :] = plane
 
-    def operator(e, write):
+    def operator(e, planes, write):
         message = zrecv[e]
-        for i in range(NX):
+        for i in planes:
             value = ex[e, 2 + i, inner, :]
             z_up, z_down = shifted_z(value, message, i, 2)
             total = coef[0, i] * value
@@ -273,20 +275,18 @@
             for step in range(1, count):
                 red_copy(k, stage, step, peer(step), mine).wait_send()
 
-    def partial_dots():
-        sums = [None] * N_DOT
-        for i in range(NX):
-            r, w, p, s, t = r_[i], w_[i], p_[i], s_[i], t_[i]
-            kp = s + SIGMA * p
-            kr = w + SIGMA * r
-            kkp = (t + SIGMA * s) + SIGMA * kp
-            terms = (
-                r * r, r * kp, r * kr, r * kkp, kp * kp, kp * kr, kp * kkp,
-                kr * kr, kr * kkp, kkp * kkp, p * kp, p * kr, p * kkp,
-            )
-            for j, term in enumerate(terms):
-                folded = term.reshape(TILES, 8, NZ).sum(axis=0)
-                sums[j] = folded if i == 0 else sums[j] + folded
+    def add_dots(sums, r, w, p, s, t):
+        kp = s + SIGMA * p
+        kr = w + SIGMA * r
+        kkp = (t + SIGMA * s) + SIGMA * kp
+        terms = (
+            r * r, r * kp, r * kr, r * kkp, kp * kp, kp * kr, kp * kkp,
+            kr * kr, kr * kkp, kkp * kkp, p * kp, p * kr, p * kkp,
+        )
+        folded = [term.reshape(TILES, 8, NZ).sum(axis=0) for term in terms]
+        return folded if sums is None else [a + b for a, b in zip(sums, folded)]
+
+    def row_of(sums):
         rows = [jnp.sum(a, axis=0, keepdims=True) for a in sums]
         rows = jnp.concatenate(rows + [jnp.zeros((16 - N_DOT, NZ), F32)], axis=0)
         sums = jnp.broadcast_to(jnp.sum(rows, axis=1, keepdims=True), (16, NZ))
@@ -420,8 +420,8 @@
     finish(E_TAN, 1)
     finish(E_SY, 1, x=False, z=False)
     message_s, message_t = zrecv[E_SX], zrecv[E_TAN]
-    packed = jnp.zeros((8, NZ), F32)
-    for i in range(NX):
+    packed = zeros
+    for i in OUTSIDE + INSIDE:
         up, down = shifted_z(s_z[i], message_s, i, 1)
         total = (ex[E_SX, 3 + i, inner, :] - ex[E_SX, 1 + i, inner, :]) * 0.5
         total += (ex[E_SY, 2 + i, 9 : 9 + NY, :] - ex[E_SY, 2 + i, 7 : 7 + NY, :]) * 0.5
@@ -433,8 +433,10 @@
         p_[i] = rhs
         x_[i] = jnp.zeros((NY, NZ), F32)
         u_[i] = jnp.zeros((NY, NZ), F32)
+        if i == OUTSIDE[-1]:
+            start(E_R, 2, y=False, z=False)
     zsend[E_R] = packed
-    start(E_R, 2)
+    start(E_R, 2, x=False)
     for i in range(NX):
         up, down = shifted_z(ex[E_TAN, 2 + i, inner, :], message_t, i, 1)
         z_up, z_down = masked(up, keep_up_1) * 0.25, masked(down, keep_down_1) * 0.25
@@ -445,64 +447,57 @@
         coef[3, i], coef[4, i] = y_up, y_down
         coef[5, i], coef[6, i] = masked(z_up, keep_up_2), masked(z_down, keep_down_2)
 
-    class Packer:
-        def __init__(self):
-            self.packed = jnp.zeros((8, NZ), F32)
-
-        def add(self, plane, i):
-            self.packed = pack_plane(self.packed, plane, i)
-
-    finish(E_R, 2)
-    pack = Packer()
+    def step(e, target, write, between=lambda: None):
+        box = [zeros]
+
+        def store(i, value):
+            put(target, i, value)
+            write(i, value)
+            box[0] = pack_plane(box[0], value, i)
+
+        finish(e, 2, x=False)
+        operator(e, INSIDE, store)
+        between()
+        finish(e, 2, y=False, z=False)
+        operator(e, OUTSIDE, store)
+        start(target, 2, y=False, z=False)
+        zsend[target] = box[0]
+        start(target, 2, x=False)
 
     def write_w(i, value):
-        put(E_W, i, value)
         w_[i] = value
         s_[i] = value
-        pack.add(value, i)
-
-    operator(E_R, write_w)
-    zsend[E_W] = pack.packed
-    start(E_W, 2)
-    finish(E_W, 2)
-    pack_t = Packer()
 
     def write_z(i, value):
-        put(E_T, i, value)
         z_[i] = value
         t_[i] = value
-        pack_t.add(value, i)
-
-    operator(E_W, write_z)
-    zsend[E_T] = pack_t.packed
+
+    step(E_R, E_W, write_w)
+    step(E_W, E_T, write_z)
+    sums = None
+    for i in range(NX):
+        sums = add_dots(sums, r_[i], w_[i], p_[i], s_[i], t_[i])
+    red_start(0, 0, row_of(sums))
 
     def block(k, beta):
         e_t, e_u = E_T + 2 * k, E_T + 2 * k + 1
-        start(e_t, 2)
-        red_start(k, 0, partial_dots())
-        red_start(k, 1, red_finish(k, 0))
-        finish(e_t, 2)
-        pack_u = Packer()
 
         def write_u(i, value):
-            put(e_u, i, value)
             z2_[i] = value - beta * u_[i]
             u_[i] = value
-            pack_u.add(value, i)
-
-        operator(e_t, write_u)
-        zsend[e_u] = pack_u.packed
-        start(e_u, 2)
-        finish(e_u, 2)
+
+        step(e_t, e_u, write_u, lambda: red_start(k, 1, red_finish(k, 0)))
 
         def write_v(i, value):
             v_[i] = value
 
-        operator(e_u, write_v)
+        finish(e_u, 2, x=False)
+        operator(e_u, INSIDE, write_v)
         alpha, beta_1, alpha_1, beta_2 = scalars(red_finish(k, 1))
-        pack_n = Packer()
-        tangents = []
-        for i in range(NX):
+        box = [zeros]
+        sums = None
+
+        def update(i):
             p, s, t, u = p_[i], s_[i], t_[i], u_[i]
             x = x_[i] + alpha * p
             r = r_[i] - alpha * (s + SIGMA * p)
@@ -518,26 +513,35 @@
             w = w - alpha_1 * (t + SIGMA * s)
             z = z - alpha_1 * (u + SIGMA * t)
             r_[i], w_[i], z_[i], u_[i] = r, w, z, u
-            p_[i] = r + beta_2 * p
-            s_[i] = w + beta_2 * s
+            p = r + beta_2 * p
+            s = w + beta_2 * s
             t = z + beta_2 * t
-            t_[i] = t
-            tangents.append(t)
-        for i in range(NX):
-            pack_n.add(tangents[i], i)
+            p_[i], s_[i], t_[i] = p, s, t
+            put(e_t + 2, i, t)
+            box[0] = pack_plane(box[0], t, i)
+
+        for i in INSIDE:
+            update(i)
+            sums = add_dots(sums, r_[i], w_[i], p_[i], s_[i], t_[i])
+        finish(e_u, 2, y=False, z=False)
+        operator(e_u, OUTSIDE, write_v)
+        for i in OUTSIDE:
+            update(i)
 
         @pl.when(k < 2)
         def _():
-            for i in range(NX):
-                put(e_t + 2, i, tangents[i])
-            zsend[e_t + 2] = pack_n.packed
-
+            start(e_t + 2, 2, y=False, z=False)
+            zsend[e_t + 2] = box[0]
+            start(e_t + 2, 2, x=False)
+
+        for i in OUTSIDE:
+            sums = add_dots(sums, r_[i], w_[i], p_[i], s_[i], t_[i])
+        red_start(k + 1, 0, row_of(sums))
         return beta_2
 
     lax.fori_loop(0, 3, block, jnp.zeros((NY, NZ), F32))
 
     last = N_RED - 1
-    red_start(last, 0, partial_dots())
     red_start(last, 1, red_finish(last, 0))
     alpha, beta_1, alpha_1, _ = scalars(red_finish(last, 1))
     for i in range(NX):
@@ -547,8 +551,9 @@
         w = w_[i] - alpha * (t + SIGMA * s)
         p = r + beta_1 * p
         s = w + beta_1 * s
-        field_out[i] = ex[E_DISP, 2 + i, inner, :] + (x + alpha_1 * p)
-        residual_out[i] = r - alpha_1 * (s + SIGMA * p)
+        gain_out[i] = x + alpha_1 * p
+        residual_out[i] = r
+        change_out[i] = alpha_1 * (s + SIGMA * p)
 
     drain(E_DISP, 1)
     drain(E_SX, 1, y=False)
@@ -574,11 +579,11 @@
     field = pltpu.VMEM(shape, F32)
     ints = pltpu.VMEM(shape, jnp.int32)
     whole = pl.BlockSpec(memory_space=pltpu.VMEM)
-    return pl.pallas_call(
+    gain, residual, change = pl.pallas_call(
         newton_kernel,
-        out_shape=(jax.ShapeDtypeStruct(shape, F32), jax.ShapeDtypeStruct(shape, F32)),
+        out_shape=(jax.ShapeDtypeStruct(shape, F32),) * 3,
         in_specs=[pl.BlockSpec(memory_space=pl.ANY)] * 9,
-        out_specs=(whole, whole),
+        out_specs=(whole,) * 3,
         scratch_shapes=[
             field,
             field,
@@ -587,7 +592,7 @@
             pltpu.VMEM((3, FAMILIES, MODES), F32),
             pltpu.VMEM((3, FAMILIES, MODES), BF16),
             pltpu.VMEM((FAMILIES, MODES), F32),
-            pltpu.VMEM((N_EX, NX + 4, NY + 16, NZ), F32),
+            pltpu.VMEM((N_EX + 1, NX + 4, NY + 16, NZ), F32),
             pltpu.VMEM((N_EX, 8, NZ), F32),
             pltpu.VMEM((N_EX, 8, NZ), F32),
             pltpu.VMEM((N_RED, 2, 16, 1, NZ), F32),
@@ -611,6 +616,7 @@
         ),
         name="newton_step",
     )(displacement, load_field, foundation, flags, slots, family_in, family_mid, family_out, family_tan)
+    return displacement + gain, residual - change
 
 
 def solution(mesh):

time: 94 us -> 92.3 us (0.982)
  other arithmetic: 0 us -> 2.29 us
  local copies, waits for them, and re-layouts: 2.26 us -> 0.01 us
  Pallas kernels: 90.9 us -> 89.1 us
    unnamed x4 -> x6, local copies, waits for them, and re-layouts: 2.26 us -> 0.01 us
    pallas_call x1, Pallas kernels: 90.9 us -> 89.1 us  [body(): pl.pallas_call(newton_kernel, out_shape=(jax.ShapeDtypeStruct(shape, F32)...]
    add x0 -> x1, other arithmetic: none -> 1.62 us  [body(): return (displacement + gain, residual - change)]
where the time goes in v3:
time: 92.3 us; the launch traced here: 92.1 us
  Pallas kernels  89.1 us (97%)
  other arithmetic  2.29 us (2%)
    pallas_call x1, Pallas kernels, body(): pl.pallas_call(newton_kernel, out_shape=(jax.ShapeDtypeStruct(shape, F32)...  89.1 us

profile of v3, /device:TPU:0, one launch (start us, length us, event | category | flops | bytes accessed | tf_op | source)
XLA Modules:
  0.0 92.1 jit_solution(1869408382661337816)
XLA Ops:
  0.6 0.0 copy-start
  0.6 89.1 %newton_step.1 = (f32[8,32,128]{2,1,0:T(8,128)}, f32[8,32,128]{2,1,0:T(8,128)}, f32[8,32,128]{2,1,0:T(8,128)}) custom-call(f32[8,32,128]{2,1,0:T(8,128)} %disp_hbm.1, f32[8,32,128]{2,1,0:T(8,128)} %load_hbm.1, f32[8,32,128]{2,1,0:T(8,128)} %found_hbm.1, s32[8,32,128]{2,1,0:T(8,128)} %flags_hbm.1, s32[8,32,128]{2,1,0:T(8,128)} %slot_hbm.1, ...), custom_call_target="tpu_custom_call" | custom-call | tf_op jit(solution)/shard_map/newton_step/pallas_call | solution.py:582
  89.8 0.0 copy-done
  89.8 0.0 copy-start.1
  89.8 0.0 copy-start.2
  89.8 1.6 %add.3 = f32[8,32,128]{2,1,0:T(8,128)} add(f32[8,32,128]{2,1,0:T(8,128)S(1)} %copy-done, f32[8,32,128]{2,1,0:T(8,128)} %get-tuple-element.5) | non-fusion elementwise | flops 32768 | bytes 393216 | tf_op jit(solution)/shard_map/add | solution.py:619
  91.4 0.0 copy-done.1
  91.4 0.0 copy-done.2
  91.4 0.7 sub.3
Async XLA Ops:
  0.6 89.2 %copy-start = (f32[8,32,128]{2,1,0:T(8,128)S(1)}, f32[8,32,128]{2,1,0:T(8,128)}, u32[]{:S(2)}) copy-start(f32[8,32,128]{2,1,0:T(8,128)} %disp_hbm.1) | copy-start | bytes 393220
  89.8 1.6 %copy-start.1 = (f32[8,32,128]{2,1,0:T(8,128)S(1)}, f32[8,32,128]{2,1,0:T(8,128)}, u32[]{:S(2)}) copy-start(f32[8,32,128]{2,1,0:T(8,128)} %get-tuple-element.6) | copy-start | bytes 393220
  89.8 1.6 %copy-start.2 = (f32[8,32,128]{2,1,0:T(8,128)S(1)}, f32[8,32,128]{2,1,0:T(8,128)}, u32[]{:S(2)}) copy-start(f32[8,32,128]{2,1,0:T(8,128)} %get-tuple-element.7) | copy-start | bytes 393220

commit v4 on v3

--- a/solution.py
+++ b/solution.py
@@ -41,8 +41,7 @@
     w_out[:, MODES:] = jnp.concatenate(tangent, axis=0).astype(BF16)
 
 
-def fibre_chunk(points, w_in, w_mid, w_out, bases):
-    places = [base + 8 * i for base in bases for i in range(8)]
+def fibre_chunk(points, w_in, w_mid, w_out, places):
     width = len(places) * NZ
     rows = jnp.concatenate([points[pl.ds(place, 8), :] for place in places], axis=1)
     family, flag = rows[6:7, :], rows[7:8, :]
@@ -312,18 +311,18 @@
 
     zeros = jnp.zeros((8, NZ), F32)
 
-    def strains_at(i, top, count, halo):
-        rows = pl.ds(8 + top, count)
-        value = ex[E_DISP, 2 + i, rows, :]
+    def strains_at(i, halo):
+        value = ex[E_DISP, 2 + i, inner, :]
         if halo is None:
+            y_up, y_down = pltpu.roll(value, NY - 1, 0), pltpu.roll(value, 1, 0)
             z_up, z_down = pltpu.roll(value, NZ - 1, 1), pltpu.roll(value, 1, 1)
         else:
+            y_up, y_down = ex[E_DISP, 2 + i, 9 : 9 + NY, :], ex[E_DISP, 2 + i, 7 : 7 + NY, :]
             z_up, z_down = shifted_z(value, halo, i, 1)
-        z_up, z_down = masked(z_up, keep_up_1), masked(z_down, keep_down_1)
         return (
-            (ex[E_DISP, 3 + i, rows, :] - ex[E_DISP, 1 + i, rows, :]) * 0.5,
-            (ex[E_DISP, 2 + i, 9 + top : 9 + top + count, :] - ex[E_DISP, 2 + i, 7 + top : 7 + top + count, :]) * 0.5,
-            (z_up - z_down) * 0.5,
+            (ex[E_DISP, 3 + i, inner, :] - ex[E_DISP, 1 + i, inner, :]) * 0.5,
+            (y_up - y_down) * 0.5,
+            (masked(z_up, keep_up_1) - masked(z_down, keep_down_1)) * 0.5,
         )
 
     def store_points(base, count, strains, family, flag):
@@ -332,16 +331,23 @@
         for k, row in enumerate(rows):
             points[pl.ds(base + k, count, stride=8), :] = row
 
-    def traits(i, top, count):
-        family = lax.shift_right_logical(slot_ref[i, top : top + count, :], CAP_SHIFT).astype(F32)
-        return family, flags_ref[i, top : top + count, :].astype(F32)
-
-    def chunks(first, last, place):
+    def traits(i):
+        family = lax.shift_right_logical(slot_ref[i], CAP_SHIFT).astype(F32)
+        return family, flags_ref[i].astype(F32)
+
+    def chunks(first, last, size, start_of):
         def chunk(j, carry):
-            fibre_chunk(points, w_in, w_mid, w_out, [pl.multiple_of(base, 64) for base in place(j)])
+            fibre_chunk(points, w_in, w_mid, w_out, [start_of(j * size + i) for i in range(size)])
             return carry
 
         lax.fori_loop(first, last, chunk, 0)
+
+    def inner_row(m):
+        plane = lax.div(m, NY - 2) + 1
+        return pl.multiple_of((plane * NY + lax.rem(m, NY - 2) + 1) * 8, 8)
+
+    def face_row(m):
+        return pl.multiple_of((m + lax.div(m, NY) * ((NX - 2) * NY)) * 8, 8)
 
     middle = range(1, NX - 1)
     loads[0].wait()
@@ -353,38 +359,29 @@
         c.wait()
     prepare_weights(fin_ref, fout_ref, ftan_ref, w_in, w_out)
     for i in middle:
-        store_points((i * NY + 8) * 8, 16, strains_at(i, 8, 16, None), *traits(i, 8, 16))
+        store_points(i * NY * 8, NY, strains_at(i, None), *traits(i))
+
+    chunks(0, 1, 32, inner_row)
     pl.semaphore_wait(barrier, len(friends))
     start(E_DISP, 1)
-
-    def middle_rows(j):
-        return j * (NY * 8) + 64, j * (NY * 8) + 128
-
-    chunks(1, 4, middle_rows)
+    chunks(1, 3, 32, inner_row)
     finish(E_DISP, 1)
     message = zrecv[E_DISP]
     edges = [zeros] * 5
     for i in range(NX):
-        strains = strains_at(i, 0, NY, message)
-        family, flag = traits(i, 0, NY)
-        columns = strains + (family, flag)
+        columns = strains_at(i, message) + traits(i)
         edges = [pack_plane(e, c, i, 1) for e, c in zip(edges, columns)]
-        for top in (0, 8, 16, 24):
-            if i in (0, NX - 1) or top in (0, 24):
-                part = [c[top : top + 8] for c in columns]
-                store_points((i * NY + top) * 8, 8, part[:3], part[3], part[4])
+        if i in middle:
+            for y in (0, NY - 1):
+                part = [c[y : y + 1] for c in columns]
+                store_points((i * NY + y) * 8, 1, part[:3], part[3], part[4])
+        else:
+            store_points(i * NY * 8, NY, columns[:3], columns[3], columns[4])
     store_points(FIX, 8, edges[:3], edges[3], edges[4])
-    fibre_chunk(points, w_in, w_mid, w_out, [FIX])
-
-    def face_rows(j):
-        base = lax.div(j, 2) * ((NX - 1) * NY * 8) + lax.rem(j, 2) * 128
-        return base, base + 64
-
-    def side_rows(j):
-        return j * (NY * 8), j * (NY * 8) + 192
-
-    chunks(0, 4, face_rows)
-    chunks(1, NX - 1, side_rows)
+    sides = [(i * NY + y) * 8 for i in middle for y in (0, NY - 1)]
+    rest = [((NX - 2) * NY + y) * 8 for y in range(NY - 5, NY - 1)]
+    fibre_chunk(points, w_in, w_mid, w_out, [FIX + 8 * i for i in range(8)] + sides + rest)
+    chunks(0, 2, 32, face_row)
 
     def results(base, count):
         sx, sy, sz, high, low = [points[pl.ds(base + k, count, stride=8), :] for k in range(5)]
@@ -401,18 +398,27 @@
     zsend[E_SX] = edges[2]
     zsend[E_TAN] = edges[3]
     for i in range(NX):
-        for top, count in ((0, NY),) if i in (0, NX - 1) else ((0, 8), (24, 8)):
-            keep_results(i, top, count, results((i * NY + top) * 8, count))
+        if i in middle:
+            for y in (0, NY - 1):
+                keep_results(i, y, 1, results((i * NY + y) * 8, 1))
+        else:
+            keep_results(i, 0, NY, results(i * NY * 8, NY))
     start(E_SX, 1, y=False)
     start(E_TAN, 1)
     start(E_SY, 1, x=False, z=False)
-    chunks(4, NX - 1, middle_rows)
+    chunks(0, 2, 40, lambda m: inner_row(m + 96))
+    drain(E_TAN, 1, x=False, z=False)
+    drain(E_SY, 1, x=False, z=False)
     for i in middle:
-        for top in (8, 16):
-            n = i * TILES + top // 8
-            values = results((i * NY + top) * 8, 8)
-            values = [jnp.where(edge_own, pltpu.roll(e, NZ - n, 1), v) for e, v in zip(edges, values)]
-            keep_results(i, top, 8, values)
+        values = results(i * NY * 8, NY)
+        columns = []
+        for e, v in zip(edges, values):
+            tiles = [
+                jnp.where(edge_own, pltpu.roll(e, NZ - (i * TILES + q), 1), v[8 * q : 8 * q + 8])
+                for q in range(TILES)
+            ]
+            columns.append(jnp.concatenate(tiles, axis=0))
+        keep_results(i, 0, NY, columns)
 
     loads[10].wait()
     loads[11].wait()
@@ -557,8 +563,7 @@
 
     drain(E_DISP, 1)
     drain(E_SX, 1, y=False)
-    drain(E_TAN, 1)
-    drain(E_SY, 1, x=False, z=False)
+    drain(E_TAN, 1, y=False)
 
     def drain_step(e, carry):
         drain(e, 2)

time: 92.3 us -> 90.8 us (0.984)
  Pallas kernels: 89.1 us -> 87.7 us
    pallas_call x1, Pallas kernels: 89.1 us -> 87.7 us  [body(): pl.pallas_call(newton_kernel, out_shape=(jax.ShapeDtypeStruct(shape, F32)...]
where the time goes in v4:
time: 90.8 us; the launch traced here: 90.6 us
  Pallas kernels  87.7 us (97%)
  other arithmetic  2.29 us (3%)
    pallas_call x1, Pallas kernels, body(): pl.pallas_call(newton_kernel, out_shape=(jax.ShapeDtypeStruct(shape, F32)...  87.7 us

profile of v4, /device:TPU:0, one launch (start us, length us, event | category | flops | bytes accessed | tf_op | source)
XLA Modules:
  0.0 90.6 jit_solution(4813471013757150494)
XLA Ops:
  0.6 0.0 copy-start
  0.6 87.7 %newton_step.1 = (f32[8,32,128]{2,1,0:T(8,128)}, f32[8,32,128]{2,1,0:T(8,128)}, f32[8,32,128]{2,1,0:T(8,128)}) custom-call(f32[8,32,128]{2,1,0:T(8,128)} %disp_hbm.1, f32[8,32,128]{2,1,0:T(8,128)} %load_hbm.1, f32[8,32,128]{2,1,0:T(8,128)} %found_hbm.1, s32[8,32,128]{2,1,0:T(8,128)} %flags_hbm.1, s32[8,32,128]{2,1,0:T(8,128)} %slot_hbm.1, ...), custom_call_target="tpu_custom_call" | custom-call | tf_op jit(solution)/shard_map/newton_step/pallas_call | solution.py:587
  88.3 0.0 copy-done
  88.3 0.0 copy-start.1
  88.3 0.0 copy-start.2
  88.3 1.6 %add.3 = f32[8,32,128]{2,1,0:T(8,128)} add(f32[8,32,128]{2,1,0:T(8,128)S(1)} %copy-done, f32[8,32,128]{2,1,0:T(8,128)} %get-tuple-element.5) | non-fusion elementwise | flops 32768 | bytes 393216 | tf_op jit(solution)/shard_map/add | solution.py:624
  90.0 0.0 copy-done.1
  90.0 0.0 copy-done.2
  90.0 0.7 sub.3
Async XLA Ops:
  0.6 87.7 %copy-start = (f32[8,32,128]{2,1,0:T(8,128)S(1)}, f32[8,32,128]{2,1,0:T(8,128)}, u32[]{:S(2)}) copy-start(f32[8,32,128]{2,1,0:T(8,128)} %disp_hbm.1) | copy-start | bytes 393220
  88.3 1.6 %copy-start.1 = (f32[8,32,128]{2,1,0:T(8,128)S(1)}, f32[8,32,128]{2,1,0:T(8,128)}, u32[]{:S(2)}) copy-start(f32[8,32,128]{2,1,0:T(8,128)} %get-tuple-element.6) | copy-start | bytes 393220
  88.3 1.6 %copy-start.2 = (f32[8,32,128]{2,1,0:T(8,128)S(1)}, f32[8,32,128]{2,1,0:T(8,128)}, u32[]{:S(2)}) copy-start(f32[8,32,128]{2,1,0:T(8,128)} %get-tuple-element.7) | copy-start | bytes 393220

commit v5 on v4

--- a/solution.py
+++ b/solution.py
@@ -72,7 +72,7 @@
 
 def newton_kernel(
     disp_hbm, load_hbm, found_hbm, flags_hbm, slot_hbm, fin_hbm, fmid_hbm, fout_hbm, ftan_hbm,
-    gain_out, residual_out, change_out,
+    field_out, residual_out, change_out,
     load_ref, found_ref, flags_ref, slot_ref, fin_ref, fout_ref, ftan_ref,
     ex, zsend, zrecv, red, points, w_in, w_mid, w_out, coef, s_z,
     x_, r_, w_, z_, z2_, p_, s_, t_, u_, v_,
@@ -355,11 +355,13 @@
     for i in range(NX):
         packed = pack_plane(packed, ex[E_DISP, 2 + i, inner, :], i, 1)
     zsend[E_DISP] = packed
-    for c in loads[1:10]:
+    loads[1].wait()
+    loads[2].wait()
+    for i in middle:
+        store_points(i * NY * 8, NY, strains_at(i, None), *traits(i))
+    for c in loads[3:10]:
         c.wait()
     prepare_weights(fin_ref, fout_ref, ftan_ref, w_in, w_out)
-    for i in middle:
-        store_points(i * NY * 8, NY, strains_at(i, None), *traits(i))
 
     chunks(0, 1, 32, inner_row)
     pl.semaphore_wait(barrier, len(friends))
@@ -557,9 +559,10 @@
         w = w_[i] - alpha * (t + SIGMA * s)
         p = r + beta_1 * p
         s = w + beta_1 * s
-        gain_out[i] = x + alpha_1 * p
+        change = alpha_1 * (s + SIGMA * p)
+        field_out[i] = (ex[E_DISP, 2 + i, inner, :] + (x + alpha_1 * p)) + change
         residual_out[i] = r
-        change_out[i] = alpha_1 * (s + SIGMA * p)
+        change_out[i] = change
 
     drain(E_DISP, 1)
     drain(E_SX, 1, y=False)
@@ -584,7 +587,7 @@
     field = pltpu.VMEM(shape, F32)
     ints = pltpu.VMEM(shape, jnp.int32)
     whole = pl.BlockSpec(memory_space=pltpu.VMEM)
-    gain, residual, change = pl.pallas_call(
+    field_and_change, residual, change = pl.pallas_call(
         newton_kernel,
         out_shape=(jax.ShapeDtypeStruct(shape, F32),) * 3,
         in_specs=[pl.BlockSpec(memory_space=pl.ANY)] * 9,
@@ -621,7 +624,7 @@
         ),
         name="newton_step",
     )(displacement, load_field, foundation, flags, slots, family_in, family_mid, family_out, family_tan)
-    return displacement + gain, residual - change
+    return field_and_change - change, residual - change
 
 
 def solution(mesh):

time: 90.8 us -> 90.1 us (level)
    add x1 -> x0, other arithmetic: 1.62 us -> none  [body(): return (displacement + gain, residual - change)]
    sub x1, other arithmetic: 0.67 us -> 1.76 us  [body(): return (field_and_change - change, residual - change)]
where the time goes in v5:
time: 90.1 us; the launch traced here: 89.9 us
  Pallas kernels  87.5 us (97%)
  other arithmetic  1.76 us (2%)
    pallas_call x1, Pallas kernels, body(): pl.pallas_call(newton_kernel, out_shape=(jax.ShapeDtypeStruct(shape, F32)...  87.5 us

profile of v5, /device:TPU:0, one launch (start us, length us, event | category | flops | bytes accessed | tf_op | source)
XLA Modules:
  0.0 89.9 jit_solution(18126733863743146327)
XLA Ops:
  0.6 87.5 %newton_step.1 = (f32[8,32,128]{2,1,0:T(8,128)}, f32[8,32,128]{2,1,0:T(8,128)}, f32[8,32,128]{2,1,0:T(8,128)}) custom-call(f32[8,32,128]{2,1,0:T(8,128)} %disp_hbm.1, f32[8,32,128]{2,1,0:T(8,128)} %load_hbm.1, f32[8,32,128]{2,1,0:T(8,128)} %found_hbm.1, s32[8,32,128]{2,1,0:T(8,128)} %flags_hbm.1, s32[8,32,128]{2,1,0:T(8,128)} %slot_hbm.1, ...), custom_call_target="tpu_custom_call" | custom-call | tf_op jit(solution)/shard_map/newton_step/pallas_call | solution.py:590
  88.2 1.8 %fusion = (f32[8,32,128]{2,1,0:T(8,128)}, f32[8,32,128]{2,1,0:T(8,128)}) fusion(f32[8,32,128]{2,1,0:T(8,128)} %get-tuple-element.7, f32[8,32,128]{2,1,0:T(8,128)} %get-tuple-element.6, f32[8,32,128]{2,1,0:T(8,128)} %get-tuple-element.5), kind=kLoop, calls=%fused_computation | loop fusion | flops 65536 | bytes 655360 | tf_op jit(solution)/shard_map/sub | solution.py:627

commit v6 on v5

--- a/solution.py
+++ b/solution.py
@@ -343,7 +343,8 @@
         lax.fori_loop(first, last, chunk, 0)
 
     def inner_row(m):
-        plane = lax.div(m, NY - 2) + 1
+        n = lax.div(m, NY - 2)
+        plane = n + 1 + 2 * lax.div(n, 2) - 6 * lax.div(n, 4)
         return pl.multiple_of((plane * NY + lax.rem(m, NY - 2) + 1) * 8, 8)
 
     def face_row(m):
@@ -381,7 +382,7 @@
             store_points(i * NY * 8, NY, columns[:3], columns[3], columns[4])
     store_points(FIX, 8, edges[:3], edges[3], edges[4])
     sides = [(i * NY + y) * 8 for i in middle for y in (0, NY - 1)]
-    rest = [((NX - 2) * NY + y) * 8 for y in range(NY - 5, NY - 1)]
+    rest = [(4 * NY + y) * 8 for y in range(NY - 5, NY - 1)]
     fibre_chunk(points, w_in, w_mid, w_out, [FIX + 8 * i for i in range(8)] + sides + rest)
     chunks(0, 2, 32, face_row)
 
@@ -408,10 +409,10 @@
     start(E_SX, 1, y=False)
     start(E_TAN, 1)
     start(E_SY, 1, x=False, z=False)
-    chunks(0, 2, 40, lambda m: inner_row(m + 96))
+    chunks(0, 1, 40, lambda m: inner_row(m + 96))
     drain(E_TAN, 1, x=False, z=False)
     drain(E_SY, 1, x=False, z=False)
-    for i in middle:
+    def take_plane(i):
         values = results(i * NY * 8, NY)
         columns = []
         for e, v in zip(edges, values):
@@ -422,6 +423,9 @@
             columns.append(jnp.concatenate(tiles, axis=0))
         keep_results(i, 0, NY, columns)
 
+    for i in (1, 2, 5, 6):
+        take_plane(i)
+
     loads[10].wait()
     loads[11].wait()
     finish(E_SX, 1, y=False)
@@ -430,6 +434,10 @@
     message_s, message_t = zrecv[E_SX], zrecv[E_TAN]
     packed = zeros
     for i in OUTSIDE + INSIDE:
+        if i == INSIDE[0]:
+            chunks(0, 1, 40, lambda m: inner_row(m + 136))
+            take_plane(3)
+            take_plane(4)
         up, down = shifted_z(s_z[i], message_s, i, 1)
         total = (ex[E_SX, 3 + i, inner, :] - ex[E_SX, 1 + i, inner, :]) * 0.5
         total += (ex[E_SY, 2 + i, 9 : 9 + NY, :] - ex[E_SY, 2 + i, 7 : 7 + NY, :]) * 0.5

time: 90.1 us -> 89.1 us (0.989)
    pallas_call x1, Pallas kernels: 87.5 us -> 86.6 us  [body(): pl.pallas_call(newton_kernel, out_shape=(jax.ShapeDtypeStruct(shape, F32)...]
where the time goes in v6:
time: 89.1 us; the launch traced here: 89 us
  Pallas kernels  86.6 us (97%)
  other arithmetic  1.76 us (2%)
    pallas_call x1, Pallas kernels, body(): pl.pallas_call(newton_kernel, out_shape=(jax.ShapeDtypeStruct(shape, F32)...  86.6 us

profile of v6, /device:TPU:0, one launch (start us, length us, event | category | flops | bytes accessed | tf_op | source)
XLA Modules:
  0.0 89.0 jit_solution(12656340747351120279)
XLA Ops:
  0.6 86.6 %newton_step.1 = (f32[8,32,128]{2,1,0:T(8,128)}, f32[8,32,128]{2,1,0:T(8,128)}, f32[8,32,128]{2,1,0:T(8,128)}) custom-call(f32[8,32,128]{2,1,0:T(8,128)} %disp_hbm.1, f32[8,32,128]{2,1,0:T(8,128)} %load_hbm.1, f32[8,32,128]{2,1,0:T(8,128)} %found_hbm.1, s32[8,32,128]{2,1,0:T(8,128)} %flags_hbm.1, s32[8,32,128]{2,1,0:T(8,128)} %slot_hbm.1, ...), custom_call_target="tpu_custom_call" | custom-call | tf_op jit(solution)/shard_map/newton_step/pallas_call | solution.py:598
  87.2 1.8 %fusion = (f32[8,32,128]{2,1,0:T(8,128)}, f32[8,32,128]{2,1,0:T(8,128)}) fusion(f32[8,32,128]{2,1,0:T(8,128)} %get-tuple-element.7, f32[8,32,128]{2,1,0:T(8,128)} %get-tuple-element.6, f32[8,32,128]{2,1,0:T(8,128)} %get-tuple-element.5), kind=kLoop, calls=%fused_computation | loop fusion | flops 65536 | bytes 655360 | tf_op jit(solution)/shard_map/sub | solution.py:635
